TPU v7x, 256 devices: a whole 4x4x8 slice. The times are simulated.
256 devices in a mesh: gx: 16 (over z_lo, x), gy: 2 (over core), gz: 8 (over z_hi, y).
Axes of the slice: x: 4, y: 4, z: 8 (z_hi: 2, z_lo: 4; z = z_hi * 4 + z_lo), core: 2. Of those that a mesh axis runs over, the one named last changes fastest.
Arguments:
- tokens: bfloat16 [128, 32, 128, 192], P('gx', 'gy', 'gz'), may hold values from -6 to 6
- upstream: bfloat16 [128, 32, 128, 192], P('gx', 'gy', 'gz'), may hold values from -6 to 6
- norm_gain: float32 [192], replicated, may hold values from 0.25 to 1.75
- norm_bias: float32 [192], replicated, may hold values from -3 to 3
- qkv_weight: bfloat16 [192, 576], replicated, may hold values from -4 to 4, as said below
- qkv_bias: float32 [576], replicated, may hold values from -3 to 3
- proj_weight: bfloat16 [192, 192], replicated, may hold values from -0.4375 to 0.4375
Outputs:
- token_grad: bfloat16 [128, 32, 128, 192], P('gx', 'gy', 'gz')
- qkv_weight_grad: float32 [192, 576], replicated
- qkv_bias_grad: float32 [576], replicated
- proj_weight_grad: float32 [192, 192], replicated
- proj_bias_grad: float32 [192], replicated
- gain_grad: float32 [192], replicated
- norm_bias_grad: float32 [192], replicated
Inputs may be any that keep to these rules, and one draw needn't show every extreme that they name: `qkv_weight`: columns are the query, key and value projections in that order, each 6 heads of 32 columns.
All inputs are finite; a program needn't handle non-finite values.
Results may differ from a plain program's by a relative error of at most 0.02.
The roundings to bfloat16 on the way count: a program that leaves them out, or rounds other values in their place, can miss the bound.
Values may be sent and summed in bfloat16 or wider, within the bound.
No kernel may reach another device: no remote copies, remote signals or barrier semaphores. Data moves between devices by JAX's collectives and lax.ppermute only.
A program may use at most 64 MiB of HBM per device.

v0:
```python
import jax
import jax.numpy as jnp
from jax import lax
from jax.sharding import PartitionSpec as P

HEADS = 6
WIN = 8
SHIFT = 4


def passed_along(value, axis, steps):
    count = lax.axis_size(axis)
    pairs = [(source, (source + steps) % count) for source in range(count)]
    return lax.ppermute(value, axis, pairs)


def window_grads(tok, upward, idents, norm_gain, norm_bias, qkv_weight, qkv_bias, proj_weight):
    length = tok.shape[0]
    width = tok.shape[1]
    heads = HEADS
    head_size = width // heads
    single = jnp.float32
    factor = head_size ** (-0.5)
    inputs = tok.astype(single)
    centred = inputs - jnp.mean(inputs, axis=-1, keepdims=True)
    inverse = lax.rsqrt(jnp.mean(centred * centred, axis=-1, keepdims=True) + 1e-05)
    normed = centred * inverse
    hidden = (normed * norm_gain + norm_bias).astype(jnp.bfloat16)
    packed = (jnp.dot(hidden, qkv_weight, preferred_element_type=single) + qkv_bias).astype(
        jnp.bfloat16
    )
    query = packed[:, :width].reshape(length, heads, head_size)
    keyset = packed[:, width : 2 * width].reshape(length, heads, head_size)
    valset = packed[:, 2 * width :].reshape(length, heads, head_size)
    scores = jnp.einsum("qhd,khd->hqk", query, keyset, preferred_element_type=single) * factor
    same = idents[:, None] == idents[None, :]
    scores = jnp.where(same[None], scores, -1e30)
    peak = jnp.max(scores, axis=-1, keepdims=True)
    expo = jnp.exp(scores - peak)
    probs = expo / jnp.sum(expo, axis=-1, keepdims=True)
    probs_half = probs.astype(jnp.bfloat16)
    attended = jnp.einsum("hqk,khd->qhd", probs_half, valset, preferred_element_type=single)
    attended = attended.reshape(length, width).astype(jnp.bfloat16)
    grad_proj = jnp.einsum("lc,lf->cf", attended, upward, preferred_element_type=single)
    grad_pbias = jnp.sum(upward.astype(single), axis=0)
    attended_grad = jnp.einsum(
        "lf,cf->lc", upward, proj_weight, preferred_element_type=single
    ).astype(jnp.bfloat16)
    attended_grad = attended_grad.reshape(length, heads, head_size)
    prob_grad = jnp.einsum("qhd,khd->hqk", attended_grad, valset, preferred_element_type=single)
    inner = jnp.sum(probs * prob_grad, axis=-1, keepdims=True)
    score_grad = (probs * (prob_grad - inner) * factor).astype(jnp.bfloat16)
    query_grad = jnp.einsum(
        "hqk,khd->qhd", score_grad, keyset, preferred_element_type=single
    ).reshape(length, width)
    key_grad = jnp.einsum("hqk,qhd->khd", score_grad, query, preferred_element_type=single).reshape(
        length, width
    )
    value_grad = jnp.einsum(
        "hqk,qhd->khd", probs_half, attended_grad, preferred_element_type=single
    ).reshape(length, width)
    packed_grad = jnp.concatenate([query_grad, key_grad, value_grad], axis=1).astype(jnp.bfloat16)
    grad_qkv = jnp.einsum("lc,lf->cf", hidden, packed_grad, preferred_element_type=single)
    grad_qbias = jnp.sum(packed_grad.astype(single), axis=0)
    hidden_grad = jnp.einsum("lf,cf->lc", packed_grad, qkv_weight, preferred_element_type=single)
    grad_gain = jnp.sum(hidden_grad * normed, axis=0)
    grad_nbias = jnp.sum(hidden_grad, axis=0)
    normed_grad = hidden_grad * norm_gain
    first = jnp.mean(normed_grad, axis=-1, keepdims=True)
    second = jnp.mean(normed_grad * normed, axis=-1, keepdims=True)
    token_grad = (upward.astype(single) + inverse * (normed_grad - first - normed * second)).astype(
        jnp.bfloat16
    )
    return (token_grad, (grad_qkv, grad_qbias, grad_proj, grad_pbias, grad_gain, grad_nbias))


def to_windows(block):
    sizes = block.shape[:3]
    rest = block.shape[3:]
    shaped = block.reshape(
        (sizes[0] // WIN, WIN, sizes[1] // WIN, WIN, sizes[2] // WIN, WIN) + rest
    )
    order = (0, 2, 4, 1, 3, 5) + tuple(range(6, 6 + len(rest)))
    return shaped.transpose(order).reshape((-1, WIN**3) + rest)


def from_windows(wins, first, second, third):
    rest = wins.shape[2:]
    shaped = wins.reshape((first // WIN, second // WIN, third // WIN, WIN, WIN, WIN) + rest)
    order = (0, 3, 1, 4, 2, 5) + tuple(range(6, 6 + len(rest)))
    return shaped.transpose(order).reshape((first, second, third) + rest)


def move_first(pieces):
    sent = passed_along((pieces[0][:SHIFT], pieces[1][:SHIFT]), "gx", -1)
    return (
        jnp.concatenate([pieces[0][SHIFT:], sent[0]], axis=0),
        jnp.concatenate([pieces[1][SHIFT:], sent[1]], axis=0),
    )


def move_second(pieces):
    sent = passed_along((pieces[0][:, :SHIFT], pieces[1][:, :SHIFT]), "gy", -1)
    return (
        jnp.concatenate([pieces[0][:, SHIFT:], sent[0]], axis=1),
        jnp.concatenate([pieces[1][:, SHIFT:], sent[1]], axis=1),
    )


def move_third(pieces):
    sent = passed_along((pieces[0][:, :, :SHIFT], pieces[1][:, :, :SHIFT]), "gz", -1)
    return (
        jnp.concatenate([pieces[0][:, :, SHIFT:], sent[0]], axis=2),
        jnp.concatenate([pieces[1][:, :, SHIFT:], sent[1]], axis=2),
    )


def window_index(count, position, length):
    total = length * count
    rolled = position * length + jnp.arange(length, dtype=jnp.int32)
    placed = (rolled + SHIFT) % total
    return ((placed + SHIFT) // WIN, total // WIN + 1, count)


def per_device(tokens, upstream, norm_gain, norm_bias, qkv_weight, qkv_bias, proj_weight):
    pieces = (tokens, upstream)
    pieces = move_third(move_second(move_first(pieces)))
    rolled, rolled_up = pieces
    depth_x, depth_y, depth_z, width = tokens.shape
    index_x, span_x, count_x = window_index(lax.axis_size("gx"), lax.axis_index("gx"), depth_x)
    index_y, span_y, count_y = window_index(lax.axis_size("gy"), lax.axis_index("gy"), depth_y)
    index_z, span_z, count_z = window_index(lax.axis_size("gz"), lax.axis_index("gz"), depth_z)
    idents = (index_x[:, None, None] * span_y + index_y[None, :, None]) * span_z + index_z[
        None, None, :
    ]
    token_wins = to_windows(rolled)
    up_wins = to_windows(rolled_up)
    ident_wins = to_windows(idents)
    zeros = (
        jnp.zeros((width, 3 * width), jnp.float32),
        jnp.zeros((3 * width,), jnp.float32),
        jnp.zeros((width, width), jnp.float32),
        jnp.zeros((width,), jnp.float32),
        jnp.zeros((width,), jnp.float32),
        jnp.zeros((width,), jnp.float32),
    )

    def advance(carry, item):
        grad_win, parts = window_grads(
            item[0], item[1], item[2], norm_gain, norm_bias, qkv_weight, qkv_bias, proj_weight
        )
        return (tuple((old + new for old, new in zip(carry, parts))), grad_win)

    totals, grad_wins = lax.scan(advance, zeros, (token_wins, up_wins, ident_wins))
    token_grad = from_windows(grad_wins, depth_x, depth_y, depth_z)
    summed = lax.psum(
        (totals[0], totals[1], totals[2], totals[3], totals[4], totals[5]), ("gx", "gy", "gz")
    )
    factor = float(depth_x * depth_y * depth_z * count_x * count_y * count_z) ** (-0.5)
    return (
        token_grad,
        summed[0] * factor,
        summed[1] * factor,
        summed[2] * factor,
        summed[3] * factor,
        summed[4] * factor,
        summed[5] * factor,
    )


def solution(mesh):
    placed = (P("gx", "gy", "gz", None), P("gx", "gy", "gz", None), P(), P(), P(), P(), P())
    return jax.shard_map(
        per_device,
        mesh=mesh,
        in_specs=placed,
        out_specs=(P("gx", "gy", "gz", None), P(), P(), P(), P(), P(), P()),
        check_vma=False,
    )
```

profile of v0, /device:TPU:1, one launch (start us, length us, event | category | flops | bytes accessed | tf_op | source)
XLA Modules:
  0.0 495.4 jit_solution(13295949907634760316)
XLA Ops:
  7.2 1.3 fusion.78
  8.5 7.4 %collective-permute-start = (bf16[4,16,16,192]{3,2,1,0:T(8,128)(2,1)S(1)}, bf16[4,16,16,192]{3,2,1,0:T(8,128)(2,1)S(1)}, u32[]{:S(2)}, u32[]{:S(2)}) collective-permute-start(bf16[4,16,16,192]{3,2,1,0:T(8,128)(2,1)S(1)} %get-tuple-element.238), channel_id=1, source_target_pairs={{0,240},{16,0},{32,16},{48,32},{64,48},{80,64},{96,80},{112,96},{1... | collective-permute-start | bytes 1179656 | tf_op jit(solution)/shard_map/ppermute | solution.py:14
  16.0 1.3 fusion.77
  17.3 0.6 collective-permute-start.3
  18.3 8.2 %collective-permute-done = bf16[4,16,16,192]{3,2,1,0:T(8,128)(2,1)S(1)} collective-permute-done((bf16[4,16,16,192]{3,2,1,0:T(8,128)(2,1)S(1)}, bf16[4,16,16,192]{3,2,1,0:T(8,128)(2,1)S(1)}, u32[]{:S(2)}, u32[]{:S(2)}) %collective-permute-start) | collective-permute-done | bytes 393248 | tf_op jit(solution)/shard_map/ppermute | solution.py:14
  26.6 2.8 collective-permute-start.1
  29.4 8.4 %collective-permute-done.3 = bf16[4,16,16,192]{3,2,1,0:T(8,128)(2,1)S(1)} collective-permute-done((bf16[4,16,16,192]{3,2,1,0:T(8,128)(2,1)S(1)}, bf16[4,16,16,192]{3,2,1,0:T(8,128)(2,1)S(1)}, u32[]{:S(2)}, u32[]{:S(2)}) %collective-permute-start.3) | collective-permute-done | bytes 393248 | tf_op jit(solution)/shard_map/ppermute | solution.py:14
  37.8 1.6 collective-permute-start.4
  39.9 6.7 %collective-permute-start.2 = (bf16[8,16,4,192]{3,2,1,0:T(4,128)(2,1)S(1)}, bf16[8,16,4,192]{3,2,1,0:T(4,128)(2,1)S(1)}, u32[]{:S(2)}, u32[]{:S(2)}) collective-permute-start(bf16[8,16,4,192]{3,2,1,0:T(4,128)(2,1)S(1)} %pad_maximum_fusion.7), channel_id=1, source_target_pairs={{0,7},{1,0},{2,1},{3,2},{4,3},{5,4},{6,5},{7,6},{8,15},{9,8},{10,9... | collective-permute-start | bytes 589832 | tf_op jit(solution)/shard_map/ppermute | solution.py:14
  46.6 0.8 pad_maximum_fusion.5
  47.4 0.7 collective-permute-start.5
  48.8 10.7 %collective-permute-done.2 = bf16[8,16,4,192]{3,2,1,0:T(4,128)(2,1)S(1)} collective-permute-done((bf16[8,16,4,192]{3,2,1,0:T(4,128)(2,1)S(1)}, bf16[8,16,4,192]{3,2,1,0:T(4,128)(2,1)S(1)}, u32[]{:S(2)}, u32[]{:S(2)}) %collective-permute-start.2) | collective-permute-done | bytes 196640 | tf_op jit(solution)/shard_map/ppermute | solution.py:14
  60.2 0.7 copy.36
  60.9 6.3 %collective-permute-done.5 = bf16[8,16,4,192]{3,2,1,0:T(4,128)(2,1)} collective-permute-done((bf16[8,16,4,192]{3,2,1,0:T(4,128)(2,1)}, bf16[8,16,4,192]{3,2,1,0:T(4,128)(2,1)}, u32[]{:S(2)}, u32[]{:S(2)}) %collective-permute-start.5) | collective-permute-done | bytes 196640 | tf_op jit(solution)/shard_map/ppermute | solution.py:14
  67.2 1.4 pad_maximum_fusion.4
  69.3 158.2 %while.23 = (s32[]{:T(128)}, f32[192,576]{1,0:T(8,128)S(1)}, f32[576]{0:T(1024)S(1)}, f32[192,192]{1,0:T(8,128)S(1)}, f32[192]{0:T(256)S(1)}, /*index=5*/f32[192...) while((s32[]{:T(128)}, f32[192,576]{1,0:T(8,128)S(1)}, ...), condition=%wide.region_12.13_spmd.clone, body=%wide.region_0.12_spmd.clone.sunk | while | flops 1065100416 | bytes 87224056 | solution.py:154
  70.0 1.4 fusion.144
  71.4 5.1 %fusion.146 = (f32[6,512]{1,0:T(8,128)S(1)}, f32[6,512,512]{1,2,0:T(8,128)}) fusion(pred[512,512]{0,1:T(8,128)(4,1)S(1)} %broadcast_compare_fusion.2, bf16[512,6,32]{0,2,1:T(8,128)(2,1)S(1)} %bitcast.162, bf16[512,6,32]{0,2,1:T(8,128)(2,1)S(1)} %bitcast.164), kind=kOutput, calls=%fused_computation.127.clone.1 | convolution fusion | flops 106955264 | bytes 6959104 | tf_op jit(solution)/shard_map/while/body/eval_jaxpr/sub | solution.py:39
  76.5 3.6 fusion.151
  80.4 0.7 copy-done.7
  81.1 1.0 fusion.147
  82.2 3.7 fusion.148
  85.9 10.8 %fusion.150 = bf16[6,32,512]{2,1,0:T(8,128)(2,1)S(1)} fusion(bf16[512,6,32]{0,2,1:T(8,128)(2,1)S(1)} %bitcast.165, f32[6,512,512]{1,2,0:T(8,128)} %fusion.148, f32[6,512,512]{1,2,0:T(8,128)} %get-tuple-element.353, f32[6,512]{1,0:T(8,128)S(1)} %get-tuple-element.354), kind=kOutput, calls=%fused_computation.22.clone.1 | convolution fusion | flops 111775232 | bytes 12988416 | tf_op jit(solution)/shard_map/while/body/eval_jaxpr/hqk,khd->qhd/dot_general | solution.py:53
  96.7 9.3 %fusion.149 = bf16[6,32,512]{2,1,0:T(8,128)(2,1)S(1)} fusion(bf16[512,6,32]{0,2,1:T(8,128)(2,1)S(1)} %bitcast.163, f32[6,512,512]{1,2,0:T(8,128)} %fusion.148, f32[6,512,512]{1,2,0:T(8,128)} %get-tuple-element.353, f32[6,512]{1,0:T(8,128)S(1)} %get-tuple-element.354), kind=kOutput, calls=%fused_computation.23.clone.1 | convolution fusion | flops 111775232 | bytes 12988416 | tf_op jit(solution)/shard_map/while/body/eval_jaxpr/hqk,qhd->khd/dot_general | solution.py:56
  106.1 1.4 fusion.152
  108.1 0.8 fusion.153
  109.5 1.4 fusion.144
  111.0 5.1 %fusion.146 = (f32[6,512]{1,0:T(8,128)S(1)}, f32[6,512,512]{1,2,0:T(8,128)}) fusion(pred[512,512]{0,1:T(8,128)(4,1)S(1)} %broadcast_compare_fusion.2, bf16[512,6,32]{0,2,1:T(8,128)(2,1)S(1)} %bitcast.162, bf16[512,6,32]{0,2,1:T(8,128)(2,1)S(1)} %bitcast.164), kind=kOutput, calls=%fused_computation.127.clone.1 | convolution fusion | flops 106955264 | bytes 6959104 | tf_op jit(solution)/shard_map/while/body/eval_jaxpr/sub | solution.py:39
  116.1 3.6 fusion.151
  120.0 0.7 copy-done.7
  120.7 1.0 fusion.147
  121.7 3.7 fusion.148
  125.4 10.8 %fusion.150 = bf16[6,32,512]{2,1,0:T(8,128)(2,1)S(1)} fusion(bf16[512,6,32]{0,2,1:T(8,128)(2,1)S(1)} %bitcast.165, f32[6,512,512]{1,2,0:T(8,128)} %fusion.148, f32[6,512,512]{1,2,0:T(8,128)} %get-tuple-element.353, f32[6,512]{1,0:T(8,128)S(1)} %get-tuple-element.354), kind=kOutput, calls=%fused_computation.22.clone.1 | convolution fusion | flops 111775232 | bytes 12988416 | tf_op jit(solution)/shard_map/while/body/eval_jaxpr/hqk,khd->qhd/dot_general | solution.py:53
  136.2 9.3 %fusion.149 = bf16[6,32,512]{2,1,0:T(8,128)(2,1)S(1)} fusion(bf16[512,6,32]{0,2,1:T(8,128)(2,1)S(1)} %bitcast.163, f32[6,512,512]{1,2,0:T(8,128)} %fusion.148, f32[6,512,512]{1,2,0:T(8,128)} %get-tuple-element.353, f32[6,512]{1,0:T(8,128)S(1)} %get-tuple-element.354), kind=kOutput, calls=%fused_computation.23.clone.1 | convolution fusion | flops 111775232 | bytes 12988416 | tf_op jit(solution)/shard_map/while/body/eval_jaxpr/hqk,qhd->khd/dot_general | solution.py:56
  145.7 1.4 fusion.152
  147.6 0.8 fusion.153
  149.1 1.4 fusion.144
  150.5 5.1 %fusion.146 = (f32[6,512]{1,0:T(8,128)S(1)}, f32[6,512,512]{1,2,0:T(8,128)}) fusion(pred[512,512]{0,1:T(8,128)(4,1)S(1)} %broadcast_compare_fusion.2, bf16[512,6,32]{0,2,1:T(8,128)(2,1)S(1)} %bitcast.162, bf16[512,6,32]{0,2,1:T(8,128)(2,1)S(1)} %bitcast.164), kind=kOutput, calls=%fused_computation.127.clone.1 | convolution fusion | flops 106955264 | bytes 6959104 | tf_op jit(solution)/shard_map/while/body/eval_jaxpr/sub | solution.py:39
  155.6 3.6 fusion.151
  159.5 0.7 copy-done.7
  160.2 1.0 fusion.147
  161.3 3.7 fusion.148
  165.0 10.8 %fusion.150 = bf16[6,32,512]{2,1,0:T(8,128)(2,1)S(1)} fusion(bf16[512,6,32]{0,2,1:T(8,128)(2,1)S(1)} %bitcast.165, f32[6,512,512]{1,2,0:T(8,128)} %fusion.148, f32[6,512,512]{1,2,0:T(8,128)} %get-tuple-element.353, f32[6,512]{1,0:T(8,128)S(1)} %get-tuple-element.354), kind=kOutput, calls=%fused_computation.22.clone.1 | convolution fusion | flops 111775232 | bytes 12988416 | tf_op jit(solution)/shard_map/while/body/eval_jaxpr/hqk,khd->qhd/dot_general | solution.py:53
  175.8 9.3 %fusion.149 = bf16[6,32,512]{2,1,0:T(8,128)(2,1)S(1)} fusion(bf16[512,6,32]{0,2,1:T(8,128)(2,1)S(1)} %bitcast.163, f32[6,512,512]{1,2,0:T(8,128)} %fusion.148, f32[6,512,512]{1,2,0:T(8,128)} %get-tuple-element.353, f32[6,512]{1,0:T(8,128)S(1)} %get-tuple-element.354), kind=kOutput, calls=%fused_computation.23.clone.1 | convolution fusion | flops 111775232 | bytes 12988416 | tf_op jit(solution)/shard_map/while/body/eval_jaxpr/hqk,qhd->khd/dot_general | solution.py:56
  185.2 1.4 fusion.152
  187.1 0.8 fusion.153
  188.6 1.4 fusion.144
  190.1 5.1 %fusion.146 = (f32[6,512]{1,0:T(8,128)S(1)}, f32[6,512,512]{1,2,0:T(8,128)}) fusion(pred[512,512]{0,1:T(8,128)(4,1)S(1)} %broadcast_compare_fusion.2, bf16[512,6,32]{0,2,1:T(8,128)(2,1)S(1)} %bitcast.162, bf16[512,6,32]{0,2,1:T(8,128)(2,1)S(1)} %bitcast.164), kind=kOutput, calls=%fused_computation.127.clone.1 | convolution fusion | flops 106955264 | bytes 6959104 | tf_op jit(solution)/shard_map/while/body/eval_jaxpr/sub | solution.py:39
  195.2 3.6 fusion.151
  199.0 0.7 copy-done.7
  199.8 1.0 fusion.147
  200.8 3.7 fusion.148
  204.5 10.8 %fusion.150 = bf16[6,32,512]{2,1,0:T(8,128)(2,1)S(1)} fusion(bf16[512,6,32]{0,2,1:T(8,128)(2,1)S(1)} %bitcast.165, f32[6,512,512]{1,2,0:T(8,128)} %fusion.148, f32[6,512,512]{1,2,0:T(8,128)} %get-tuple-element.353, f32[6,512]{1,0:T(8,128)S(1)} %get-tuple-element.354), kind=kOutput, calls=%fused_computation.22.clone.1 | convolution fusion | flops 111775232 | bytes 12988416 | tf_op jit(solution)/shard_map/while/body/eval_jaxpr/hqk,khd->qhd/dot_general | solution.py:53
  215.3 9.3 %fusion.149 = bf16[6,32,512]{2,1,0:T(8,128)(2,1)S(1)} fusion(bf16[512,6,32]{0,2,1:T(8,128)(2,1)S(1)} %bitcast.163, f32[6,512,512]{1,2,0:T(8,128)} %fusion.148, f32[6,512,512]{1,2,0:T(8,128)} %get-tuple-element.353, f32[6,512]{1,0:T(8,128)S(1)} %get-tuple-element.354), kind=kOutput, calls=%fused_computation.23.clone.1 | convolution fusion | flops 111775232 | bytes 12988416 | tf_op jit(solution)/shard_map/while/body/eval_jaxpr/hqk,qhd->khd/dot_general | solution.py:56
  224.8 1.4 fusion.152
  226.7 0.8 fusion.153
  227.5 0.7 copy-done
  228.4 81.4 %all-reduce = (f32[576]{0:T(1024)S(1)}, f32[192]{0:T(256)S(1)}, f32[192]{0:T(256)S(1)}, f32[192]{0:T(256)S(1)}) all-reduce(f32[576]{0:T(1024)S(1)} %get-tuple-element.97, f32[192]{0:T(256)S(1)} %get-tuple-element.99, f32[192]{0:T(256)S(1)} %get-tuple-element.100, ...), channel_id=1, replica_groups=mesh['gx'=16,'gy'=2,'gz'=8] {'gx','gy','gz'}, use_global_device_ids=true, to_apply=%region_14.15 | all-reduce | flops 1152 | bytes 9216 | tf_op jit(solution)/shard_map/psum | solution.py:156
  310.9 1.4 copy.38
  312.3 1.1 copy.39
  313.4 0.6 broadcast_multiply_fusion.5
  314.0 171.1 %all-reduce.4.cloned.1.call-done = (f32[192,576]{1,0:T(8,128)}, f32[192,192]{1,0:T(8,128)}) async-done(((f32[192,576]{1,0:T(8,128)}, f32[192,192]{1,0:T(8,128)}), (f32[192,576]{1,0:T(8,128)}, f32[192,192]{1,0:T(8,128)})) %all-reduce.4.cloned.1.call-update) | async-done | bytes 589840 | tf_op jit(solution)/shard_map/psum | solution.py:156
  485.1 1.9 broadcast_multiply_fusion.3
  486.9 1.6 broadcast_multiply_fusion.4
  (115 shorter events, 10.4 us)
Async XLA Ops:
  7.2 477.9 %all-reduce.4.cloned.1.call-start = ((), (), s32[]{:S(2)}) async-start(), calls=%async_computation | async-start | bytes 1376256 | tf_op jit(solution)/shard_map/psum | solution.py:156
  8.5 18.0 %collective-permute-start = (bf16[4,16,16,192]{3,2,1,0:T(8,128)(2,1)S(1)}, bf16[4,16,16,192]{3,2,1,0:T(8,128)(2,1)S(1)}, u32[]{:S(2)}, u32[]{:S(2)}) collective-permute-start(bf16[4,16,16,192]{3,2,1,0:T(8,128)(2,1)S(1)} %get-tuple-element.238), channel_id=1, source_target_pairs={{0,240},{16,0},{32,16},{48,32},{64,48},{80,64},{96,80},{112,96},{1... | collective-permute-start | bytes 1179656 | tf_op jit(solution)/shard_map/ppermute | solution.py:14
  17.3 20.5 %collective-permute-start.3 = (bf16[4,16,16,192]{3,2,1,0:T(8,128)(2,1)S(1)}, bf16[4,16,16,192]{3,2,1,0:T(8,128)(2,1)S(1)}, u32[]{:S(2)}, u32[]{:S(2)}) collective-permute-start(bf16[4,16,16,192]{3,2,1,0:T(8,128)(2,1)S(1)} %get-tuple-element.236), channel_id=1, source_target_pairs={{0,240},{16,0},{32,16},{48,32},{64,48},{80,64},{96,80},{112,96},{1... | collective-permute-start | bytes 1179656 | tf_op jit(solution)/shard_map/ppermute | solution.py:14
  26.6 13.1 %collective-permute-start.1 = (bf16[8,4,16,192]{3,2,1,0:T(8,128)(2,1)S(1)}, bf16[8,4,16,192]{3,2,1,0:T(8,128)(2,1)S(1)}, u32[]{:S(2)}, u32[]{:S(2)}) collective-permute-start(bf16[8,4,16,192]{3,2,1,0:T(8,128)(2,1)S(1)} %pad_maximum_fusion.8), channel_id=1, source_target_pairs={{0,8},{8,0},{1,9},{9,1},{2,10},{10,2},{3,11},{11,3},{4,12},{12,4},... | collective-permute-start | bytes 589832 | tf_op jit(solution)/shard_map/ppermute | solution.py:14
  37.8 8.8 %collective-permute-start.4 = (bf16[8,4,16,192]{3,2,1,0:T(8,128)(2,1)S(1)}, bf16[8,4,16,192]{3,2,1,0:T(8,128)(2,1)S(1)}, u32[]{:S(2)}, u32[]{:S(2)}) collective-permute-start(bf16[8,4,16,192]{3,2,1,0:T(8,128)(2,1)S(1)} %pad_maximum_fusion.6), channel_id=1, source_target_pairs={{0,8},{8,0},{1,9},{9,1},{2,10},{10,2},{3,11},{11,3},{4,12},{12,4},... | collective-permute-start | bytes 589832 | tf_op jit(solution)/shard_map/ppermute | solution.py:14
  39.9 19.6 %collective-permute-start.2 = (bf16[8,16,4,192]{3,2,1,0:T(4,128)(2,1)S(1)}, bf16[8,16,4,192]{3,2,1,0:T(4,128)(2,1)S(1)}, u32[]{:S(2)}, u32[]{:S(2)}) collective-permute-start(bf16[8,16,4,192]{3,2,1,0:T(4,128)(2,1)S(1)} %pad_maximum_fusion.7), channel_id=1, source_target_pairs={{0,7},{1,0},{2,1},{3,2},{4,3},{5,4},{6,5},{7,6},{8,15},{9,8},{10,9... | collective-permute-start | bytes 589832 | tf_op jit(solution)/shard_map/ppermute | solution.py:14
  47.4 19.8 %collective-permute-start.5 = (bf16[8,16,4,192]{3,2,1,0:T(4,128)(2,1)}, bf16[8,16,4,192]{3,2,1,0:T(4,128)(2,1)}, u32[]{:S(2)}, u32[]{:S(2)}) collective-permute-start(bf16[8,16,4,192]{3,2,1,0:T(4,128)(2,1)} %pad_maximum_fusion.5), channel_id=1, source_target_pairs={{0,7},{1,0},{2,1},{3,2},{4,3},{5,4},{6,5},{7,6},{8,15},{9,8},{10,9... | collective-permute-start | bytes 589832 | tf_op jit(solution)/shard_map/ppermute | solution.py:14
  48.7 20.6 %copy-start.1 = (bf16[192,192]{1,0:T(8,128)(2,1)S(1)}, bf16[192,192]{1,0:T(8,128)(2,1)}, u32[]{:S(2)}) copy-start(bf16[192,192]{1,0:T(8,128)(2,1)} %param.15) | copy-start | bytes 221188
  48.7 20.6 %copy-start.4 = (f32[192]{0:T(256)S(1)}, f32[192]{0:T(256)}, u32[]{:S(2)}) copy-start(f32[192]{0:T(256)} %param.11) | copy-start | bytes 2308
  48.7 20.6 %copy-start.5 = (f32[576]{0:T(1024)S(1)}, f32[576]{0:T(1024)}, u32[]{:S(2)}) copy-start(f32[576]{0:T(1024)} %param.14) | copy-start | bytes 6916
  48.8 20.6 %copy-start.6 = (f32[192]{0:T(256)S(1)}, f32[192]{0:T(256)}, u32[]{:S(2)}) copy-start(f32[192]{0:T(256)} %param.12) | copy-start | bytes 2308
  60.9 8.4 %copy-start.2 = (f32[192,576]{1,0:T(8,128)S(1)}, f32[192,576]{1,0:T(8,128)}, u32[]{:S(2)}) copy-start(f32[192,576]{1,0:T(8,128)} %custom-call) | copy-start | bytes 1327108
  76.5 4.6 copy-start.7
  116.1 4.6 copy-start.7
  155.6 4.6 copy-start.7
  195.2 4.6 copy-start.7
  227.5 0.7 copy-start
  227.5 0.8 copy-start.3
Sparse Core Ops, SparseCore 0:
  228.5 256.4 all-reduce.3
where the time goes:
time: 496 us; the launch traced here: 495 us
  waiting for transfers between devices  205 us (41%)
  matrix products  149 us (30%)
  blocking collectives  81.4 us (16%)
  starting transfers between devices  20 us (4%)
  other arithmetic  15.2 us (3%)
  between operations  14.3 us (3%)
  local copies, waits for them, and re-layouts  10.6 us (2%)
    psum x1, waiting for transfers between devices, per_device(): lax.psum((totals[0], totals[1], totals[2], totals[3], totals[4], totals[5...  171 us
    psum x1, blocking collectives, per_device(): lax.psum((totals[0], totals[1], totals[2], totals[3], totals[4], totals[5...  81.4 us
    dot_general x4, matrix products, window_grads(): jnp.einsum('hqk,khd->qhd', score_grad, keyset, preferred_element_type=sin...  43.1 us
    dot_general x4, matrix products, window_grads(): jnp.einsum('hqk,qhd->khd', score_grad, query, preferred_element_type=single)  37 us
    ppermute x6, waiting for transfers between devices, passed_along(): return lax.ppermute(value, axis, pairs)  33.7 us
    sub x4, matrix products, window_grads(): expo = jnp.exp(scores - peak)  20.4 us
    ppermute x6, starting transfers between devices, passed_along(): return lax.ppermute(value, axis, pairs)  19.9 us
    dot_general x4, matrix products, window_grads(): jnp.einsum('qhd,khd->hqk', attended_grad, valset, preferred_element_type=...  14.8 us
  transfers between devices with their start and end apart: 7, of which 5 were waited for; matrix products, arithmetic and copies ran while one was open for 2% of the time, Pallas kernels for 0%

commit v1 on v0

v1 whole, which is shorter than its diff:
```python
import functools
import math

import jax
import jax.numpy as jnp
from jax import lax
from jax.experimental import pallas as pl
from jax.experimental.pallas import tpu as pltpu
from jax.sharding import Mesh, PartitionSpec as P

HEADS = 6
WIN = 8
SHIFT = 4
FAR = -1e30
LANES = 128
F32 = jnp.float32
BF16 = jnp.bfloat16


def dot(a, b):
    return jnp.dot(a, b, preferred_element_type=F32)


def dot_rows(a, b):
    return lax.dot_general(a, b, (((1,), (1,)), ((), ())), preferred_element_type=F32)


def dot_cols(a, b):
    return lax.dot_general(a, b, (((0,), (0,)), ((), ())), preferred_element_type=F32)


def window_kernel(
    flags, tok, up, gain, nbias, w_cols, w_rows, qbias, proj,
    out, grads, acc_qkv, acc_proj, acc_gain, acc_nb, packed_grad, attended,
):
    step = pl.program_id(0)
    width = w_rows.shape[0]
    count = WIN**3
    size = width // HEADS
    factor = size**-0.5
    scale = factor * math.log2(math.e)

    @pl.when(step == 0)
    def _():
        acc_qkv[...] = jnp.zeros_like(acc_qkv)
        acc_proj[...] = jnp.zeros_like(acc_proj)
        acc_gain[...] = jnp.zeros_like(acc_gain)
        acc_nb[...] = jnp.zeros_like(acc_nb)
        attended[...] = jnp.ones_like(attended)

    upward = up[...].astype(F32).reshape(count, width)
    upward_half = upward.astype(BF16)
    inputs = tok[...].astype(F32).reshape(count, width).T
    centred = inputs - jnp.mean(inputs, axis=0, keepdims=True)
    inverse = lax.rsqrt(jnp.mean(centred * centred, axis=0, keepdims=True) + 1e-5)
    normed = centred * inverse
    hidden = (normed * gain[...] + nbias[...]).astype(BF16)
    packed = (dot(w_cols[...], hidden) + qbias[...]).astype(BF16)
    att_grad = dot_rows(proj[...], upward_half).astype(BF16)

    last = (step == pl.num_programs(0) - 1).astype(jnp.int32)
    place = lax.broadcasted_iota(jnp.int32, (16, count), 1)
    row = lax.broadcasted_iota(jnp.int32, (16, count), 0)
    code = (
        4 * flags[0] * ((place >> 8) & 1)
        + 2 * flags[1] * last * ((place >> 5) & 1)
        + flags[2] * ((place >> 2) & 1)
    )
    same = code == row
    query_code = jnp.where(same, 1.0, 0.0).astype(BF16)
    key_code = jnp.where(same, 0.0, FAR).astype(BF16)
    ones = jnp.ones((16, count), BF16)

    for head in range(HEADS):
        lo = size * head
        at_q = slice(lo, lo + size)
        at_k = slice(width + lo, width + lo + size)
        at_v = slice(2 * width + lo, 2 * width + lo + size)
        query, keyset, valset, grad = packed[at_q], packed[at_k], packed[at_v], att_grad[at_q]
        value_ones = jnp.concatenate([valset, ones], axis=0)
        scores = dot_cols(
            jnp.concatenate([keyset, key_code], axis=0),
            jnp.concatenate([query, query_code], axis=0),
        )
        peak = jnp.max(scores, axis=0, keepdims=True)
        expo = jnp.exp2(scores * scale - peak * scale).astype(BF16)
        mixed = dot(value_ones, expo)
        recip = 1.0 / mixed[size : size + 1]
        result = mixed[:size] * recip
        attended[at_q, :] = result.astype(BF16)
        grad_scaled = (grad.astype(F32) * recip).astype(BF16)
        inner = jnp.sum(grad_scaled.astype(F32) * result, axis=0, keepdims=True)
        inner_high = inner.astype(BF16).astype(F32)
        inner_rows = jnp.where(
            row == 0, -inner_high, jnp.where(row == 1, inner_high - inner, 0.0)
        ).astype(BF16)
        spread = dot_cols(value_ones, jnp.concatenate([grad_scaled, inner_rows], axis=0))
        score_grad = expo * spread.astype(BF16)
        packed_grad[at_q, :] = (dot(keyset, score_grad) * factor).astype(BF16)
        packed_grad[at_k, :] = (dot_rows(query, score_grad) * factor).astype(BF16)
        packed_grad[at_v, :] = dot_rows(grad_scaled, expo).astype(BF16)

    grad_half = packed_grad[...]
    acc_qkv[...] += dot_rows(jnp.concatenate([hidden, ones], axis=0), grad_half)
    acc_proj[...] += dot(attended[...], upward_half)
    hidden_grad = dot(w_rows[...], grad_half)
    acc_gain[...] += hidden_grad * normed
    acc_nb[...] += hidden_grad
    normed_grad = hidden_grad * gain[...]
    first = jnp.mean(normed_grad, axis=0, keepdims=True)
    second = jnp.mean(normed_grad * normed, axis=0, keepdims=True)
    change = inverse * (normed_grad - first - normed * second)
    out[...] = (upward + change.T).reshape(out.shape).astype(BF16)

    @pl.when(step == pl.num_programs(0) - 1)
    def _():
        def put(at, value):
            grads[at : at + value.shape[0], : value.shape[1]] = value

        def over_tokens(value):
            folded = value[:, :LANES]
            for j in range(1, count // LANES):
                folded = folded + value[:, j * LANES : (j + 1) * LANES]
            return jnp.sum(folded.T, axis=0, keepdims=True)

        qkv = acc_qkv[...]
        prj = acc_proj[...]
        for j in range(4):
            put(width * j, qkv[:width, j * LANES : (j + 1) * LANES])
        put(width * 4, prj[:width, :LANES])
        put(
            width * 5,
            jnp.concatenate([qkv[:width, 4 * LANES :], prj[:width, LANES:]], axis=1),
        )
        grads[width * 6 :, :] = jnp.zeros_like(grads[width * 6 :, :])
        base = width * 6
        for j in range(5):
            put(base + j, qkv[width : width + 1, j * LANES : (j + 1) * LANES])
        small = [prj[width : width + 1], over_tokens(acc_gain[...]), over_tokens(acc_nb[...])]
        for j, value in enumerate(small):
            put(base + 8 + 2 * j, value[:, :LANES])
            put(base + 9 + 2 * j, value[:, LANES:])


def windows(flags, tok, up, weights, rows):
    depth, width_y, depth_z, width = tok.shape
    count = WIN**3
    block = pl.BlockSpec((WIN, WIN, WIN, width), lambda i: (0, i, 0, 0))
    whole = lambda *shape: pl.BlockSpec(shape, lambda i: (0,) * len(shape))
    return pl.pallas_call(
        window_kernel,
        grid=(width_y // WIN,),
        in_specs=[pl.BlockSpec(memory_space=pltpu.SMEM), block, block]
        + [whole(*value.shape) for value in weights],
        out_specs=[block, whole(rows, LANES)],
        out_shape=[
            jax.ShapeDtypeStruct(tok.shape, BF16),
            jax.ShapeDtypeStruct((rows, LANES), F32),
        ],
        scratch_shapes=[
            pltpu.VMEM((width + 16, 3 * width), F32),
            pltpu.VMEM((width + 16, width), F32),
            pltpu.VMEM((width, count), F32),
            pltpu.VMEM((width, count), F32),
            pltpu.VMEM((3 * width, count), BF16),
            pltpu.VMEM((width + 16, count), BF16),
        ],
        compiler_params=pltpu.CompilerParams(vmem_limit_bytes=48 * 2**20),
        name="window_grads",
    )(flags, tok, up, *weights)


def swapped(value, axis, bit):
    count = lax.axis_size(axis)
    return lax.ppermute(value, axis, [(a, a ^ bit) for a in range(count)])


def halve(value, axis, bit):
    half = value.shape[0] // 2
    upper = (lax.axis_index(axis) // bit) % 2
    pair = value.reshape((2, half) + value.shape[1:])
    kept = lax.dynamic_index_in_dim(pair, upper, 0, keepdims=False)
    given = lax.dynamic_index_in_dim(pair, 1 - upper, 0, keepdims=False)
    return kept + swapped(given, axis, bit)


def join(value, axis, bit):
    upper = (lax.axis_index(axis) // bit) % 2
    other = swapped(value, axis, bit)
    return jnp.where(
        upper == 0,
        jnp.concatenate([value, other], axis=0),
        jnp.concatenate([other, value], axis=0),
    )


def bits_of(axis):
    return [1 << j for j in range(lax.axis_size(axis).bit_length() - 1)]


def summed_everywhere(value):
    for axis in ("c", "y"):
        for bit in bits_of(axis):
            value = halve(value, axis, bit)
    for axis in ("x", "zl", "zh"):
        for bit in bits_of(axis):
            value = value + swapped(value, axis, bit)
    for axis in ("y", "c"):
        for bit in reversed(bits_of(axis)):
            value = join(value, axis, bit)
    return value


def passed_back(value, axes):
    sizes = [lax.axis_size(axis) for axis in axes]
    count = math.prod(sizes)
    return lax.ppermute(value, axes, [(a, (a - 1) % count) for a in range(count)])


def passed_back_both(value, first, second):
    ones = [lax.axis_size(axis) for axis in first]
    twos = [lax.axis_size(axis) for axis in second]
    n, m = math.prod(ones), math.prod(twos)
    pairs = [
        (a * m + b, ((a - 1) % n) * m + (b - 1) % m) for a in range(n) for b in range(m)
    ]
    return lax.ppermute(value, first + second, pairs)


def per_device(tokens, upstream, norm_gain, norm_bias, qkv_weight, qkv_bias, proj_weight):
    gx, gy, gz = ("zl", "x"), ("c",), ("zh", "y")
    width = tokens.shape[3]
    both = jnp.stack([tokens, upstream])
    came = passed_back(both[:, :, :SHIFT], gy)
    both = jnp.concatenate([both[:, :, SHIFT:], came], axis=2)
    came_x = passed_back(both[:, :SHIFT, :, SHIFT:], gx)
    came_z = passed_back(both[:, SHIFT:, :, :SHIFT], gz)
    came_xz = passed_back_both(both[:, :SHIFT, :, :SHIFT], gx, gz)
    near = jnp.concatenate([both[:, SHIFT:, :, SHIFT:], came_x], axis=1)
    rear = jnp.concatenate([came_z, came_xz], axis=1)
    half_a = near[:, :, :, :WIN]
    half_b = jnp.concatenate([near[:, :, :, WIN:], rear], axis=3)

    def is_last(axes):
        at = jnp.int32(0)
        count = 1
        for axis in axes:
            at = at * lax.axis_size(axis) + lax.axis_index(axis)
            count *= lax.axis_size(axis)
        return (at == count - 1).astype(jnp.int32)

    last_x, last_y, last_z = is_last(gx), is_last(gy), is_last(gz)
    weights = (
        norm_gain.reshape(-1, 1),
        norm_bias.reshape(-1, 1),
        qkv_weight.T,
        qkv_weight,
        qkv_bias.reshape(-1, 1),
        proj_weight,
    )
    rows = 6 * width + 64
    out_a, grads_a = windows(
        jnp.stack([last_x, last_y, 0 * last_z]), half_a[0], half_a[1], weights, rows
    )
    out_b, grads_b = windows(
        jnp.stack([last_x, last_y, last_z]), half_b[0], half_b[1], weights, rows
    )
    token_grad = jnp.concatenate([out_a, out_b], axis=2)
    total = summed_everywhere(grads_a + grads_b)
    devices = math.prod(lax.axis_size(axis) for axis in gx + gy + gz)
    total = total * float(math.prod(tokens.shape[:3]) * devices) ** (-0.5)
    parts = [total[width * j : width * (j + 1)] for j in range(6)]
    half = width - LANES
    qkv_grad = jnp.concatenate(parts[:4] + [parts[5][:, :half]], axis=1)
    proj_grad = jnp.concatenate([parts[4], parts[5][:, half:]], axis=1)
    small = total[6 * width :]
    flat = small.reshape(-1)
    at = 8 * LANES
    return (
        token_grad,
        qkv_grad,
        flat[: 3 * width],
        proj_grad,
        flat[at : at + width],
        flat[at + 2 * LANES : at + 2 * LANES + width],
        flat[at + 4 * LANES : at + 4 * LANES + width],
    )


def solution(mesh):
    split = Mesh(mesh.devices.reshape(4, 4, 2, 2, 4), ("zl", "x", "c", "zh", "y"))
    block = P(("zl", "x"), "c", ("zh", "y"), None)
    return jax.shard_map(
        per_device,
        mesh=split,
        in_specs=(block, block, P(), P(), P(), P(), P()),
        out_specs=(block, P(), P(), P(), P(), P(), P()),
        check_vma=False,
    )
```

time: 496 us -> 159 us (0.32)
  matrix products: 149 us -> 0 us
  waiting for transfers between devices: 205 us -> 66.3 us
  blocking collectives: 81.4 us -> 0 us
  Pallas kernels: 0 us -> 36 us
  starting transfers between devices: 20 us -> 41.8 us
  between operations: 14.3 us -> 1.02 us
  other arithmetic: 15.2 us -> 6.48 us
  local copies, waits for them, and re-layouts: 10.6 us -> 5.52 us
    psum x1 -> x0, waiting for transfers between devices: 171 us -> none  [per_device(): lax.psum((totals[0], totals[1], totals[2], totals[3], totals[4], totals[5...]
    dot_general x40 -> x0, matrix products: 128 us -> none  [the longest x4 43.1 us: window_grads(): jnp.einsum('hqk,khd->qhd', score_grad, keyset, preferred_element_type=sin...]
    psum x1 -> x0, blocking collectives: 81.4 us -> none  [per_device(): lax.psum((totals[0], totals[1], totals[2], totals[3], totals[4], totals[5...]
    pallas_call x0 -> x2, Pallas kernels: none -> 36 us  [windows(): pl.pallas_call(window_kernel, grid=(width_y // WIN,), in_specs=[pl.BlockS...]
    ppermute x6 -> x15, waiting for transfers between devices: 33.7 us -> 66.3 us  [the longest x11 34.6 us: swapped(): return lax.ppermute(value, axis, [(a, a ^ bit) for a in range(count)])]
    ppermute x6 -> x15, starting transfers between devices: 19.9 us -> 41.8 us  [the longest x11 26.2 us: swapped(): return lax.ppermute(value, axis, [(a, a ^ bit) for a in range(count)])]
    sub x4 -> x0, matrix products: 20.4 us -> none  [window_grads(): expo = jnp.exp(scores - peak)]
    mul x7 -> x1, other arithmetic: 5.29 us -> 0.06 us  [per_device(): total = total * float(math.prod(tokens.shape[:3]) * devices) ** (-0.5)]
  transfers between devices with their start and end apart: 7 -> 15, of which waited for: 5 -> 14; matrix products, arithmetic and copies ran while one was open for 2% -> 3% of each run, Pallas kernels for 0% -> 0%
where the time goes in v1:
time: 159 us; the launch traced here: 157 us
  waiting for transfers between devices  66.3 us (42%)
  starting transfers between devices  41.8 us (26%)
  Pallas kernels  36 us (23%)
  other arithmetic  6.48 us (4%)
  local copies, waits for them, and re-layouts  5.52 us (3%)
    pallas_call x2, Pallas kernels, windows(): pl.pallas_call(window_kernel, grid=(width_y // WIN,), in_specs=[pl.BlockS...  36 us
    ppermute x11, waiting for transfers between devices, swapped(): return lax.ppermute(value, axis, [(a, a ^ bit) for a in range(count)])  34.6 us
    ppermute x3, waiting for transfers between devices, passed_back(): lax.ppermute(value, axes, [(a, (a - 1) % count) for a in range(count)])  31.7 us
    ppermute x11, starting transfers between devices, swapped(): return lax.ppermute(value, axis, [(a, a ^ bit) for a in range(count)])  26.2 us
    ppermute x3, starting transfers between devices, passed_back(): lax.ppermute(value, axes, [(a, (a - 1) % count) for a in range(count)])  11.3 us
    ppermute x1, starting transfers between devices, passed_back_both(): return lax.ppermute(value, first + second, pairs)  4.31 us
  transfers between devices with their start and end apart: 15, of which 14 were waited for; matrix products, arithmetic and copies ran while one was open for 3% of the time, Pallas kernels for 0%

profile of v1, /device:TPU:1, one launch (start us, length us, event | category | flops | bytes accessed | tf_op | source)
XLA Modules:
  0.0 157.2 jit_solution(4448568115856883758)
XLA Ops:
  0.6 0.0 copy-start.3
  0.6 0.0 copy-start.4
  0.7 1.3 pad_maximum_fusion.2
  1.9 3.3 %collective-permute-start = (bf16[2,8,4,16,192]{4,3,2,1,0:T(8,128)(2,1)S(1)}, bf16[2,8,4,16,192]{4,3,2,1,0:T(8,128)(2,1)S(1)}, u32[]{:S(2)}, u32[]{:S(2)}) collective-permute-start(bf16[2,8,4,16,192]{4,3,2,1,0:T(8,128)(2,1)S(1)} %pad_maximum_fusion.2), channel_id=1, source_target_pairs={{0,8},{8,0},{1,9},{9,1},{2,10},{10,2},{3,11},{11,3},{4,12},{12,4},... | collective-permute-start | bytes 1179656 | tf_op jit(solution)/shard_map/ppermute | solution.py:217
  5.3 0.0 copy-done.3
  5.3 0.0 copy-done.4
  5.3 0.3 fusion
  5.6 1.2 collective-permute-done
  6.8 1.6 %fusion.1 = (bf16[2,4,16,12,192]{4,3,2,1,0:T(8,128)(2,1)}, bf16[2,4,16,12,192]{4,3,2,1,0:T(8,128)(2,1)S(1)}) fusion(bf16[2,8,12,16,192]{4,3,2,1,0:T(8,128)(2,1)S(1)} %fusion, bf16[2,8,4,16,192]{4,3,2,1,0:T(8,128)(2,1)S(1)} %collective-permute-done), kind=kLoop, calls=%fused_computation.9 | loop fusion | flops 589824 | bytes 2752512 | tf_op jit(solution)/shard_map/concatenate | solution.py:235
  8.4 1.2 copy.22
  9.6 4.8 %collective-permute-start.1 = (bf16[2,4,16,12,192]{4,2,3,1,0:T(8,128)(2,1)}, bf16[2,4,16,12,192]{4,2,3,1,0:T(8,128)(2,1)}, u32[]{:S(2)}, u32[]{:S(2)}) collective-permute-start(bf16[2,4,16,12,192]{4,2,3,1,0:T(8,128)(2,1)} %copy.22), channel_id=1, source_target_pairs={{0,240},{16,0},{32,16},{48,32},{64,48},{80,64},{96,80},{112,96},{1... | collective-permute-start | bytes 1769480 | tf_op jit(solution)/shard_map/ppermute | solution.py:217
  14.4 0.0 copy-done.7
  14.4 0.1 copy.25.gain
  14.5 0.0 copy-done.8
  14.5 0.1 copy.26.nbias
  14.7 0.2 copy.24
  14.8 0.1 reshape.45.qbias
  15.0 0.2 fusion.5
  15.2 0.0 copy-start.2
  15.2 4.3 %collective-permute-start.3 = (bf16[2,4,16,4,192]{4,3,2,1,0:T(4,128)(2,1)S(1)}, bf16[2,4,16,4,192]{4,3,2,1,0:T(4,128)(2,1)S(1)}, u32[]{:S(2)}, u32[]{:S(2)}) collective-permute-start(bf16[2,4,16,4,192]{4,3,2,1,0:T(4,128)(2,1)S(1)} %get-tuple-element.18), channel_id=1, source_target_pairs={{0,247},{1,240},{2,241},{3,242},{4,243},{5,244},{6,245},{7,246},{1... | collective-permute-start | bytes 589832 | tf_op jit(solution)/shard_map/ppermute | solution.py:227
  19.5 3.2 %collective-permute-start.2 = (bf16[2,4,16,4,192]{4,3,2,1,0:T(4,128)(2,1)S(1)}, bf16[2,4,16,4,192]{4,3,2,1,0:T(4,128)(2,1)S(1)}, u32[]{:S(2)}, u32[]{:S(2)}) collective-permute-start(bf16[2,4,16,4,192]{4,3,2,1,0:T(4,128)(2,1)S(1)} %get-tuple-element.17), channel_id=1, source_target_pairs={{0,7},{1,0},{2,1},{3,2},{4,3},{5,4},{6,5},{7,6},{8,15},{9,8},{10,9... | collective-permute-start | bytes 589832 | tf_op jit(solution)/shard_map/ppermute | solution.py:217
  22.7 0.1 pad_add_fusion
  22.8 26.7 %collective-permute-done.1 = bf16[2,4,16,12,192]{4,2,3,1,0:T(8,128)(2,1)} collective-permute-done((bf16[2,4,16,12,192]{4,2,3,1,0:T(8,128)(2,1)}, bf16[2,4,16,12,192]{4,2,3,1,0:T(8,128)(2,1)}, u32[]{:S(2)}, u32[]{:S(2)}) %collective-permute-start.1) | collective-permute-done | bytes 589856 | tf_op jit(solution)/shard_map/ppermute | solution.py:217
  49.4 1.4 copy.23
  50.9 0.2 maximum_bitcast_fusion
  51.1 0.0 collective-permute-done.3
  51.1 3.8 %collective-permute-done.2 = bf16[2,4,16,4,192]{4,3,2,1,0:T(4,128)(2,1)S(1)} collective-permute-done((bf16[2,4,16,4,192]{4,3,2,1,0:T(4,128)(2,1)S(1)}, bf16[2,4,16,4,192]{4,3,2,1,0:T(4,128)(2,1)S(1)}, u32[]{:S(2)}, u32[]{:S(2)}) %collective-permute-start.2) | collective-permute-done | bytes 196640 | tf_op jit(solution)/shard_map/ppermute | solution.py:217
  54.9 0.6 fusion.3
  55.5 0.0 copy-start.1
  55.6 0.1 slice_bitcast_fusion
  55.6 0.8 copy-done.1
  56.4 17.9 %window_grads.3 = (bf16[8,16,8,192]{3,2,1,0:T(8,128)(2,1)S(1)}, f32[1216,128]{1,0:T(8,128)S(1)}) custom-call(s32[3]{0:T(128)S(1)} %get-tuple-element.31.flags, bf16[8,16,8,192]{3,2,1,0:T(8,128)(2,1)S(1)} %get-tuple-element.22.tok, bf16[8,16,8,192]{3,2,1,0:T(8,128)(2,1)S(1)} %get-tuple-element.21.up, f32[192,1]{1,0:T(8,128)S(1)} %copy.25.gain, ...), custom_call_target="tpu_custom_call" | custom-call | tf_op jit(solution)/shard_map/window_grads/pallas_call | solution.py:150
  74.4 18.1 %window_grads.2 = (bf16[8,16,8,192]{3,2,1,0:T(8,128)(2,1)S(1)}, f32[1216,128]{1,0:T(8,128)S(1)}) custom-call(s32[3]{0:T(128)S(1)} %get-tuple-element.30.flags, bf16[8,16,8,192]{3,2,1,0:T(8,128)(2,1)S(1)} %get-tuple-element.16.tok, bf16[8,16,8,192]{3,2,1,0:T(8,128)(2,1)S(1)} %get-tuple-element.15.up, f32[192,1]{1,0:T(8,128)S(1)} %copy.25.gain, ...), custom_call_target="tpu_custom_call" | custom-call | tf_op jit(solution)/shard_map/window_grads/pallas_call | solution.py:150
  92.5 0.1 add.78
  92.6 1.3 collective-permute-start.4
  93.9 1.2 collective-permute-done.4
  95.2 0.1 collective-permute-start.5
  95.3 5.2 %collective-permute-done.5 = f32[304,128]{1,0:T(8,128)S(1)} collective-permute-done((f32[304,128]{1,0:T(8,128)S(1)}, f32[304,128]{1,0:T(8,128)S(1)}, u32[]{:S(2)}, u32[]{:S(2)}) %collective-permute-start.5) | collective-permute-done | bytes 155680 | tf_op jit(solution)/shard_map/ppermute | solution.py:175
  100.6 6.2 %collective-permute-start.6 = (f32[152,128]{1,0:T(8,128)S(1)}, f32[152,128]{1,0:T(8,128)S(1)}, u32[]{:S(2)}, u32[]{:S(2)}) collective-permute-start(f32[152,128]{1,0:T(8,128)S(1)} %dynamic-slice_bitcast_fusion.2), channel_id=1, source_target_pairs={{0,2},{1,3},{2,0},{3,1},{4,6},{5,7},{6,4},{7,5},{8,10},{9,11},{10,... | collective-permute-start | bytes 233480 | tf_op jit(solution)/shard_map/ppermute | solution.py:175
  106.8 1.8 %collective-permute-done.6 = f32[152,128]{1,0:T(8,128)S(1)} collective-permute-done((f32[152,128]{1,0:T(8,128)S(1)}, f32[152,128]{1,0:T(8,128)S(1)}, u32[]{:S(2)}, u32[]{:S(2)}) %collective-permute-start.6) | collective-permute-done | bytes 77856 | tf_op jit(solution)/shard_map/ppermute | solution.py:175
  108.6 0.1 collective-permute-start.7
  108.7 3.2 %collective-permute-done.7 = f32[152,128]{1,0:T(8,128)S(1)} collective-permute-done((f32[152,128]{1,0:T(8,128)S(1)}, f32[152,128]{1,0:T(8,128)S(1)}, u32[]{:S(2)}, u32[]{:S(2)}) %collective-permute-start.7) | collective-permute-done | bytes 77856 | tf_op jit(solution)/shard_map/ppermute | solution.py:175
  112.0 4.8 %collective-permute-start.8 = (f32[152,128]{1,0:T(8,128)S(1)}, f32[152,128]{1,0:T(8,128)S(1)}, u32[]{:S(2)}, u32[]{:S(2)}) collective-permute-start(f32[152,128]{1,0:T(8,128)S(1)} %add.88), channel_id=1, source_target_pairs={{0,32},{16,48},{32,0},{48,16},{1,33},{17,49},{33,1},{49,17},{2,34}... | collective-permute-start | bytes 233480 | tf_op jit(solution)/shard_map/ppermute | solution.py:175
  116.8 2.3 %collective-permute-done.8 = f32[152,128]{1,0:T(8,128)S(1)} collective-permute-done((f32[152,128]{1,0:T(8,128)S(1)}, f32[152,128]{1,0:T(8,128)S(1)}, u32[]{:S(2)}, u32[]{:S(2)}) %collective-permute-start.8) | collective-permute-done | bytes 77856 | tf_op jit(solution)/shard_map/ppermute | solution.py:175
  119.1 0.1 collective-permute-start.9
  119.2 3.2 %collective-permute-done.9 = f32[152,128]{1,0:T(8,128)S(1)} collective-permute-done((f32[152,128]{1,0:T(8,128)S(1)}, f32[152,128]{1,0:T(8,128)S(1)}, u32[]{:S(2)}, u32[]{:S(2)}) %collective-permute-start.9) | collective-permute-done | bytes 77856 | tf_op jit(solution)/shard_map/ppermute | solution.py:175
  122.4 0.1 collective-permute-start.10
  122.5 4.7 %collective-permute-done.10 = f32[152,128]{1,0:T(8,128)S(1)} collective-permute-done((f32[152,128]{1,0:T(8,128)S(1)}, f32[152,128]{1,0:T(8,128)S(1)}, u32[]{:S(2)}, u32[]{:S(2)}) %collective-permute-start.10) | collective-permute-done | bytes 77856 | tf_op jit(solution)/shard_map/ppermute | solution.py:175
  127.2 0.1 collective-permute-start.11
  127.3 7.1 %collective-permute-done.11 = f32[152,128]{1,0:T(8,128)S(1)} collective-permute-done((f32[152,128]{1,0:T(8,128)S(1)}, f32[152,128]{1,0:T(8,128)S(1)}, u32[]{:S(2)}, u32[]{:S(2)}) %collective-permute-start.11) | collective-permute-done | bytes 77856 | tf_op jit(solution)/shard_map/ppermute | solution.py:175
  134.5 2.8 %collective-permute-start.12 = (f32[152,128]{1,0:T(8,128)S(1)}, f32[152,128]{1,0:T(8,128)S(1)}, u32[]{:S(2)}, u32[]{:S(2)}) collective-permute-start(f32[152,128]{1,0:T(8,128)S(1)} %add.92), channel_id=1, source_target_pairs={{0,2},{1,3},{2,0},{3,1},{4,6},{5,7},{6,4},{7,5},{8,10},{9,11},{10,... | collective-permute-start | bytes 233480 | tf_op jit(solution)/shard_map/ppermute | solution.py:175
  137.3 2.0 %collective-permute-done.12 = f32[152,128]{1,0:T(8,128)S(1)} collective-permute-done((f32[152,128]{1,0:T(8,128)S(1)}, f32[152,128]{1,0:T(8,128)S(1)}, u32[]{:S(2)}, u32[]{:S(2)}) %collective-permute-start.12) | collective-permute-done | bytes 77856 | tf_op jit(solution)/shard_map/ppermute | solution.py:175
  139.3 0.4 collective-permute-start.13
  139.8 3.8 %collective-permute-done.13 = f32[304,128]{1,0:T(8,128)S(1)} collective-permute-done((f32[304,128]{1,0:T(8,128)S(1)}, f32[304,128]{1,0:T(8,128)S(1)}, u32[]{:S(2)}, u32[]{:S(2)}) %collective-permute-start.13) | collective-permute-done | bytes 155680 | tf_op jit(solution)/shard_map/ppermute | solution.py:175
  143.5 10.2 %collective-permute-start.14 = (f32[608,128]{1,0:T(8,128)S(1)}, f32[608,128]{1,0:T(8,128)S(1)}, u32[]{:S(2)}, u32[]{:S(2)}) collective-permute-start(f32[608,128]{1,0:T(8,128)S(1)} %maximum_select_fusion.1), channel_id=1, source_target_pairs={{0,8},{8,0},{1,9},{9,1},{2,10},{10,2},{3,11},{11,3},{4,12},{12,4},... | collective-permute-start | bytes 933896 | tf_op jit(solution)/shard_map/ppermute | solution.py:175
  153.8 1.2 pad_maximum_fusion.1
  154.9 0.1 collective-permute-done.14
  155.0 0.1 fusion.4
  155.1 0.6 slice.114
  155.7 0.6 fusion.8
  156.3 0.1 fusion.7
  156.4 0.0 copy-start.5
  156.4 0.7 pad_maximum_fusion.4
  157.1 0.1 copy-done.5
  (25 shorter events, 0.3 us)
Async XLA Ops:
  0.6 4.6 %copy-start.3 = (bf16[8,16,16,192]{3,2,1,0:T(8,128)(2,1)S(1)}, bf16[8,16,16,192]{3,2,1,0:T(8,128)(2,1)}, u32[]{:S(2)}) copy-start(bf16[8,16,16,192]{3,2,1,0:T(8,128)(2,1)} %param.7) | copy-start | bytes 2359300
  0.6 4.6 %copy-start.4 = (bf16[8,16,16,192]{3,2,1,0:T(8,128)(2,1)S(1)}, bf16[8,16,16,192]{3,2,1,0:T(8,128)(2,1)}, u32[]{:S(2)}) copy-start(bf16[8,16,16,192]{3,2,1,0:T(8,128)(2,1)} %param.8) | copy-start | bytes 2359300
  1.9 4.9 %collective-permute-start = (bf16[2,8,4,16,192]{4,3,2,1,0:T(8,128)(2,1)S(1)}, bf16[2,8,4,16,192]{4,3,2,1,0:T(8,128)(2,1)S(1)}, u32[]{:S(2)}, u32[]{:S(2)}) collective-permute-start(bf16[2,8,4,16,192]{4,3,2,1,0:T(8,128)(2,1)S(1)} %pad_maximum_fusion.2), channel_id=1, source_target_pairs={{0,8},{8,0},{1,9},{9,1},{2,10},{10,2},{3,11},{11,3},{4,12},{12,4},... | collective-permute-start | bytes 1179656 | tf_op jit(solution)/shard_map/ppermute | solution.py:217
  8.4 6.0 %copy-start.7 = (f32[192]{0:T(256)S(1)}, f32[192]{0:T(256)}, u32[]{:S(2)}) copy-start(f32[192]{0:T(256)} %param.9) | copy-start | bytes 2308
  8.4 6.1 %copy-start.8 = (f32[192]{0:T(256)S(1)}, f32[192]{0:T(256)}, u32[]{:S(2)}) copy-start(f32[192]{0:T(256)} %param.10) | copy-start | bytes 2308
  8.4 6.3 %copy-start = (bf16[192,576]{1,0:T(8,128)(2,1)S(1)}, bf16[192,576]{1,0:T(8,128)(2,1)}, u32[]{:S(2)}) copy-start(bf16[192,576]{1,0:T(8,128)(2,1)} %w_rows.3) | copy-start | bytes 663556
  8.4 6.4 %copy-start.6 = (f32[576]{0:T(1024)S(1)}, f32[576]{0:T(1024)}, u32[]{:S(2)}) copy-start(f32[576]{0:T(1024)} %param.12) | copy-start | bytes 6916
  9.6 39.8 %collective-permute-start.1 = (bf16[2,4,16,12,192]{4,2,3,1,0:T(8,128)(2,1)}, bf16[2,4,16,12,192]{4,2,3,1,0:T(8,128)(2,1)}, u32[]{:S(2)}, u32[]{:S(2)}) collective-permute-start(bf16[2,4,16,12,192]{4,2,3,1,0:T(8,128)(2,1)} %copy.22), channel_id=1, source_target_pairs={{0,240},{16,0},{32,16},{48,32},{64,48},{80,64},{96,80},{112,96},{1... | collective-permute-start | bytes 1769480 | tf_op jit(solution)/shard_map/ppermute | solution.py:217
  15.2 35.7 %copy-start.2 = (bf16[2,4,16,12,192]{4,3,2,1,0:T(8,128)(2,1)S(1)}, bf16[2,4,16,12,192]{4,3,2,1,0:T(8,128)(2,1)}, u32[]{:S(2)}) copy-start(bf16[2,4,16,12,192]{4,3,2,1,0:T(8,128)(2,1)} %get-tuple-element.19) | copy-start | bytes 1769476
  15.2 35.9 %collective-permute-start.3 = (bf16[2,4,16,4,192]{4,3,2,1,0:T(4,128)(2,1)S(1)}, bf16[2,4,16,4,192]{4,3,2,1,0:T(4,128)(2,1)S(1)}, u32[]{:S(2)}, u32[]{:S(2)}) collective-permute-start(bf16[2,4,16,4,192]{4,3,2,1,0:T(4,128)(2,1)S(1)} %get-tuple-element.18), channel_id=1, source_target_pairs={{0,247},{1,240},{2,241},{3,242},{4,243},{5,244},{6,245},{7,246},{1... | collective-permute-start | bytes 589832 | tf_op jit(solution)/shard_map/ppermute | solution.py:227
  19.5 35.4 %collective-permute-start.2 = (bf16[2,4,16,4,192]{4,3,2,1,0:T(4,128)(2,1)S(1)}, bf16[2,4,16,4,192]{4,3,2,1,0:T(4,128)(2,1)S(1)}, u32[]{:S(2)}, u32[]{:S(2)}) collective-permute-start(bf16[2,4,16,4,192]{4,3,2,1,0:T(4,128)(2,1)S(1)} %get-tuple-element.17), channel_id=1, source_target_pairs={{0,7},{1,0},{2,1},{3,2},{4,3},{5,4},{6,5},{7,6},{8,15},{9,8},{10,9... | collective-permute-start | bytes 589832 | tf_op jit(solution)/shard_map/ppermute | solution.py:217
  55.5 0.9 copy-start.1
  92.6 2.5 %collective-permute-start.4 = (f32[608,128]{1,0:T(8,128)S(1)}, f32[608,128]{1,0:T(8,128)S(1)}, u32[]{:S(2)}, u32[]{:S(2)}) collective-permute-start(f32[608,128]{1,0:T(8,128)S(1)} %dynamic-slice_bitcast_fusion), channel_id=1, source_target_pairs={{0,8},{8,0},{1,9},{9,1},{2,10},{10,2},{3,11},{11,3},{4,12},{12,4},... | collective-permute-start | bytes 933896 | tf_op jit(solution)/shard_map/ppermute | solution.py:175
  95.2 5.3 %collective-permute-start.5 = (f32[304,128]{1,0:T(8,128)S(1)}, f32[304,128]{1,0:T(8,128)S(1)}, u32[]{:S(2)}, u32[]{:S(2)}) collective-permute-start(f32[304,128]{1,0:T(8,128)S(1)} %dynamic-slice_bitcast_fusion.1), channel_id=1, source_target_pairs={{0,1},{1,0},{2,3},{3,2},{4,5},{5,4},{6,7},{7,6},{8,9},{9,8},{10,11... | collective-permute-start | bytes 466952 | tf_op jit(solution)/shard_map/ppermute | solution.py:175
  100.6 8.0 %collective-permute-start.6 = (f32[152,128]{1,0:T(8,128)S(1)}, f32[152,128]{1,0:T(8,128)S(1)}, u32[]{:S(2)}, u32[]{:S(2)}) collective-permute-start(f32[152,128]{1,0:T(8,128)S(1)} %dynamic-slice_bitcast_fusion.2), channel_id=1, source_target_pairs={{0,2},{1,3},{2,0},{3,1},{4,6},{5,7},{6,4},{7,5},{8,10},{9,11},{10,... | collective-permute-start | bytes 233480 | tf_op jit(solution)/shard_map/ppermute | solution.py:175
  108.6 3.3 %collective-permute-start.7 = (f32[152,128]{1,0:T(8,128)S(1)}, f32[152,128]{1,0:T(8,128)S(1)}, u32[]{:S(2)}, u32[]{:S(2)}) collective-permute-start(f32[152,128]{1,0:T(8,128)S(1)} %bitcast_add_fusion.2), channel_id=1, source_target_pairs={{0,16},{16,0},{32,48},{48,32},{1,17},{17,1},{33,49},{49,33},{2,18}... | collective-permute-start | bytes 233480 | tf_op jit(solution)/shard_map/ppermute | solution.py:175
  112.0 7.1 %collective-permute-start.8 = (f32[152,128]{1,0:T(8,128)S(1)}, f32[152,128]{1,0:T(8,128)S(1)}, u32[]{:S(2)}, u32[]{:S(2)}) collective-permute-start(f32[152,128]{1,0:T(8,128)S(1)} %add.88), channel_id=1, source_target_pairs={{0,32},{16,48},{32,0},{48,16},{1,33},{17,49},{33,1},{49,17},{2,34}... | collective-permute-start | bytes 233480 | tf_op jit(solution)/shard_map/ppermute | solution.py:175
  119.1 3.3 %collective-permute-start.9 = (f32[152,128]{1,0:T(8,128)S(1)}, f32[152,128]{1,0:T(8,128)S(1)}, u32[]{:S(2)}, u32[]{:S(2)}) collective-permute-start(f32[152,128]{1,0:T(8,128)S(1)} %add.89), channel_id=1, source_target_pairs={{0,64},{64,0},{128,192},{192,128},{1,65},{65,1},{129,193},{193,129... | collective-permute-start | bytes 233480 | tf_op jit(solution)/shard_map/ppermute | solution.py:175
  122.4 4.8 %collective-permute-start.10 = (f32[152,128]{1,0:T(8,128)S(1)}, f32[152,128]{1,0:T(8,128)S(1)}, u32[]{:S(2)}, u32[]{:S(2)}) collective-permute-start(f32[152,128]{1,0:T(8,128)S(1)} %add.90), channel_id=1, source_target_pairs={{0,128},{64,192},{128,0},{192,64},{1,129},{65,193},{129,1},{193,65... | collective-permute-start | bytes 233480 | tf_op jit(solution)/shard_map/ppermute | solution.py:175
  127.2 7.2 %collective-permute-start.11 = (f32[152,128]{1,0:T(8,128)S(1)}, f32[152,128]{1,0:T(8,128)S(1)}, u32[]{:S(2)}, u32[]{:S(2)}) collective-permute-start(f32[152,128]{1,0:T(8,128)S(1)} %add.91), channel_id=1, source_target_pairs={{0,4},{4,0},{1,5},{5,1},{2,6},{6,2},{3,7},{7,3},{8,12},{12,8},{9,1... | collective-permute-start | bytes 233480 | tf_op jit(solution)/shard_map/ppermute | solution.py:175
  134.5 4.8 %collective-permute-start.12 = (f32[152,128]{1,0:T(8,128)S(1)}, f32[152,128]{1,0:T(8,128)S(1)}, u32[]{:S(2)}, u32[]{:S(2)}) collective-permute-start(f32[152,128]{1,0:T(8,128)S(1)} %add.92), channel_id=1, source_target_pairs={{0,2},{1,3},{2,0},{3,1},{4,6},{5,7},{6,4},{7,5},{8,10},{9,11},{10,... | collective-permute-start | bytes 233480 | tf_op jit(solution)/shard_map/ppermute | solution.py:175
  139.3 4.2 %collective-permute-start.13 = (f32[304,128]{1,0:T(8,128)S(1)}, f32[304,128]{1,0:T(8,128)S(1)}, u32[]{:S(2)}, u32[]{:S(2)}) collective-permute-start(f32[304,128]{1,0:T(8,128)S(1)} %maximum_select_fusion.2), channel_id=1, source_target_pairs={{0,1},{1,0},{2,3},{3,2},{4,5},{5,4},{6,7},{7,6},{8,9},{9,8},{10,11... | collective-permute-start | bytes 466952 | tf_op jit(solution)/shard_map/ppermute | solution.py:175
  143.5 11.4 %collective-permute-start.14 = (f32[608,128]{1,0:T(8,128)S(1)}, f32[608,128]{1,0:T(8,128)S(1)}, u32[]{:S(2)}, u32[]{:S(2)}) collective-permute-start(f32[608,128]{1,0:T(8,128)S(1)} %maximum_select_fusion.1), channel_id=1, source_target_pairs={{0,8},{8,0},{1,9},{9,1},{2,10},{10,2},{3,11},{11,3},{4,12},{12,4},... | collective-permute-start | bytes 933896 | tf_op jit(solution)/shard_map/ppermute | solution.py:175
  156.4 0.8 copy-start.5

commit v2 on v1

--- a/solution.py
+++ b/solution.py
@@ -13,6 +13,9 @@
 SHIFT = 4
 FAR = -1e30
 LANES = 128
+PARTS = 8
+MAIN = 144
+ROWS = MAIN + 8
 F32 = jnp.float32
 BF16 = jnp.bfloat16
 
@@ -30,7 +33,7 @@
 
 
 def window_kernel(
-    flags, tok, up, gain, nbias, w_cols, w_rows, qbias, proj,
+    flags, both, gain, nbias, w_cols, w_rows, qbias, proj,
     out, grads, acc_qkv, acc_proj, acc_gain, acc_nb, packed_grad, attended,
 ):
     step = pl.program_id(0)
@@ -48,9 +51,10 @@
         acc_nb[...] = jnp.zeros_like(acc_nb)
         attended[...] = jnp.ones_like(attended)
 
-    upward = up[...].astype(F32).reshape(count, width)
+    arrived = both[...].astype(F32).reshape(count, 2 * width)
+    upward = arrived[:, :width]
     upward_half = upward.astype(BF16)
-    inputs = tok[...].astype(F32).reshape(count, width).T
+    inputs = arrived[:, LANES:].T[width - LANES :]
     centred = inputs - jnp.mean(inputs, axis=0, keepdims=True)
     inverse = lax.rsqrt(jnp.mean(centred * centred, axis=0, keepdims=True) + 1e-5)
     normed = centred * inverse
@@ -115,7 +119,15 @@
     @pl.when(step == pl.num_programs(0) - 1)
     def _():
         def put(at, value):
-            grads[at : at + value.shape[0], : value.shape[1]] = value
+            done = 0
+            while done < value.shape[0]:
+                part, inside = divmod(at + done, MAIN)
+                rows = min(value.shape[0] - done, MAIN - inside)
+                grads[part, inside : inside + rows, :] = value[done : done + rows]
+                done += rows
+
+        def put_small(at, value):
+            grads[at // 2, MAIN + at % 2, : value.shape[1]] = value[0]
 
         def over_tokens(value):
             folded = value[:, :LANES]
@@ -132,30 +144,35 @@
             width * 5,
             jnp.concatenate([qkv[:width, 4 * LANES :], prj[:width, LANES:]], axis=1),
         )
-        grads[width * 6 :, :] = jnp.zeros_like(grads[width * 6 :, :])
-        base = width * 6
+        grads[:, MAIN:, :] = jnp.zeros_like(grads[:, MAIN:, :])
         for j in range(5):
-            put(base + j, qkv[width : width + 1, j * LANES : (j + 1) * LANES])
+            put_small(j, qkv[width : width + 1, j * LANES : (j + 1) * LANES])
         small = [prj[width : width + 1], over_tokens(acc_gain[...]), over_tokens(acc_nb[...])]
         for j, value in enumerate(small):
-            put(base + 8 + 2 * j, value[:, :LANES])
-            put(base + 9 + 2 * j, value[:, LANES:])
-
-
-def windows(flags, tok, up, weights, rows):
-    depth, width_y, depth_z, width = tok.shape
+            put_small(8 + 2 * j, value[:, :LANES])
+            put_small(9 + 2 * j, value[:, LANES:])
+
+
+def windows(flags, both, weights):
+    depth, width_y, depth_z, wide = both.shape
+    width = wide // 2
     count = WIN**3
-    block = pl.BlockSpec((WIN, WIN, WIN, width), lambda i: (0, i, 0, 0))
     whole = lambda *shape: pl.BlockSpec(shape, lambda i: (0,) * len(shape))
     return pl.pallas_call(
         window_kernel,
         grid=(width_y // WIN,),
-        in_specs=[pl.BlockSpec(memory_space=pltpu.SMEM), block, block]
+        in_specs=[
+            pl.BlockSpec(memory_space=pltpu.SMEM),
+            pl.BlockSpec((WIN, WIN, WIN, wide), lambda i: (0, i, 0, 0)),
+        ]
         + [whole(*value.shape) for value in weights],
-        out_specs=[block, whole(rows, LANES)],
+        out_specs=[
+            pl.BlockSpec((WIN, WIN, WIN, width), lambda i: (0, i, 0, 0)),
+            whole(PARTS, ROWS, LANES),
+        ],
         out_shape=[
-            jax.ShapeDtypeStruct(tok.shape, BF16),
-            jax.ShapeDtypeStruct((rows, LANES), F32),
+            jax.ShapeDtypeStruct((depth, width_y, depth_z, width), BF16),
+            jax.ShapeDtypeStruct((PARTS, ROWS, LANES), F32),
         ],
         scratch_shapes=[
             pltpu.VMEM((width + 16, 3 * width), F32),
@@ -166,8 +183,11 @@
             pltpu.VMEM((width + 16, count), BF16),
         ],
         compiler_params=pltpu.CompilerParams(vmem_limit_bytes=48 * 2**20),
+        cost_estimate=pl.CostEstimate(
+            flops=20 * 10**9, transcendentals=4 * 10**6, bytes_accessed=4 * 10**6
+        ),
         name="window_grads",
-    )(flags, tok, up, *weights)
+    )(flags, both, *weights)
 
 
 def swapped(value, axis, bit):
@@ -175,13 +195,28 @@
     return lax.ppermute(value, axis, [(a, a ^ bit) for a in range(count)])
 
 
+def coded(value):
+    small = value[:, MAIN:]
+    high = lax.reduce_precision(small, 8, 7)
+    return jnp.concatenate([value[:, :MAIN], high, small - high], axis=1).astype(BF16)
+
+
+def decoded(value):
+    wide = value.astype(F32)
+    small = wide[:, MAIN:ROWS] + wide[:, ROWS:]
+    return jnp.concatenate([wide[:, :MAIN], small], axis=1)
+
+
+def exchanged(value, axis, bit):
+    return decoded(swapped(coded(value), axis, bit))
+
+
 def halve(value, axis, bit):
     half = value.shape[0] // 2
     upper = (lax.axis_index(axis) // bit) % 2
-    pair = value.reshape((2, half) + value.shape[1:])
-    kept = lax.dynamic_index_in_dim(pair, upper, 0, keepdims=False)
-    given = lax.dynamic_index_in_dim(pair, 1 - upper, 0, keepdims=False)
-    return kept + swapped(given, axis, bit)
+    kept = lax.dynamic_slice_in_dim(value, upper * half, half, 0)
+    given = lax.dynamic_slice_in_dim(value, (1 - upper) * half, half, 0)
+    return kept + exchanged(given, axis, bit)
 
 
 def join(value, axis, bit):
@@ -204,11 +239,12 @@
             value = halve(value, axis, bit)
     for axis in ("x", "zl", "zh"):
         for bit in bits_of(axis):
-            value = value + swapped(value, axis, bit)
+            value = value + exchanged(value, axis, bit)
+    value = coded(value)
     for axis in ("y", "c"):
         for bit in reversed(bits_of(axis)):
             value = join(value, axis, bit)
-    return value
+    return decoded(value)
 
 
 def passed_back(value, axes):
@@ -230,16 +266,24 @@
 def per_device(tokens, upstream, norm_gain, norm_bias, qkv_weight, qkv_bias, proj_weight):
     gx, gy, gz = ("zl", "x"), ("c",), ("zh", "y")
     width = tokens.shape[3]
-    both = jnp.stack([tokens, upstream])
-    came = passed_back(both[:, :, :SHIFT], gy)
-    both = jnp.concatenate([both[:, :, SHIFT:], came], axis=2)
-    came_x = passed_back(both[:, :SHIFT, :, SHIFT:], gx)
-    came_z = passed_back(both[:, SHIFT:, :, :SHIFT], gz)
-    came_xz = passed_back_both(both[:, :SHIFT, :, :SHIFT], gx, gz)
-    near = jnp.concatenate([both[:, SHIFT:, :, SHIFT:], came_x], axis=1)
-    rear = jnp.concatenate([came_z, came_xz], axis=1)
-    half_a = near[:, :, :, :WIN]
-    half_b = jnp.concatenate([near[:, :, :, WIN:], rear], axis=3)
+    both = jnp.concatenate([upstream, tokens], axis=3)
+    a_z, b_z = slice(SHIFT, SHIFT + WIN), slice(SHIFT + WIN, None)
+    came_a = passed_back(both[:SHIFT, SHIFT:, a_z], gx)
+    came_y = passed_back(both[:, :SHIFT], gy)
+    came_ay = passed_back(came_y[:SHIFT, :, a_z], gx)
+    both = jnp.concatenate([both[:, SHIFT:], came_y], axis=1)
+    came_b = passed_back(both[:SHIFT, :, b_z], gx)
+    came_z = passed_back(both[SHIFT:, :, :SHIFT], gz)
+    came_xz = passed_back_both(both[:SHIFT, :, :SHIFT], gx, gz)
+    far = jnp.concatenate([came_a, came_ay], axis=1)
+    half_a = jnp.concatenate([both[SHIFT:, :, a_z], far], axis=0)
+    half_b = jnp.concatenate(
+        [
+            jnp.concatenate([both[SHIFT:, :, b_z], came_b], axis=0),
+            jnp.concatenate([came_z, came_xz], axis=0),
+        ],
+        axis=2,
+    )
 
     def is_last(axes):
         at = jnp.int32(0)
@@ -258,23 +302,18 @@
         qkv_bias.reshape(-1, 1),
         proj_weight,
     )
-    rows = 6 * width + 64
-    out_a, grads_a = windows(
-        jnp.stack([last_x, last_y, 0 * last_z]), half_a[0], half_a[1], weights, rows
-    )
-    out_b, grads_b = windows(
-        jnp.stack([last_x, last_y, last_z]), half_b[0], half_b[1], weights, rows
-    )
+    out_a, grads_a = windows(jnp.stack([last_x, last_y, 0 * last_z]), half_a, weights)
+    out_b, grads_b = windows(jnp.stack([last_x, last_y, last_z]), half_b, weights)
     token_grad = jnp.concatenate([out_a, out_b], axis=2)
     total = summed_everywhere(grads_a + grads_b)
     devices = math.prod(lax.axis_size(axis) for axis in gx + gy + gz)
     total = total * float(math.prod(tokens.shape[:3]) * devices) ** (-0.5)
-    parts = [total[width * j : width * (j + 1)] for j in range(6)]
+    main = total[:, :MAIN].reshape(-1, LANES)
+    parts = [main[width * j : width * (j + 1)] for j in range(6)]
     half = width - LANES
     qkv_grad = jnp.concatenate(parts[:4] + [parts[5][:, :half]], axis=1)
     proj_grad = jnp.concatenate([parts[4], parts[5][:, half:]], axis=1)
-    small = total[6 * width :]
-    flat = small.reshape(-1)
+    flat = total[:, MAIN : MAIN + 2].reshape(-1)
     at = 8 * LANES
     return (
         token_grad,

time: 159 us -> 120 us (0.75)
  waiting for transfers between devices: 66.3 us -> 25.5 us
  other arithmetic: 6.48 us -> 10.2 us
  local copies, waits for them, and re-layouts: 5.52 us -> 3.32 us
    ppermute x3 -> x5, waiting for transfers between devices: 31.7 us -> 0.01 us  [passed_back(): lax.ppermute(value, axes, [(a, (a - 1) % count) for a in range(count)])]
    ppermute x11, waiting for transfers between devices: 34.6 us -> 25.4 us  [swapped(): return lax.ppermute(value, axis, [(a, a ^ bit) for a in range(count)])]
    concatenate x3 -> x16, other arithmetic: 2.38 us -> 7.51 us  [the longest x3 3.44 us: per_device(): both = jnp.concatenate([upstream, tokens], axis=3)]
    ppermute x3 -> x5, starting transfers between devices: 11.3 us -> 12.2 us  [passed_back(): lax.ppermute(value, axes, [(a, (a - 1) % count) for a in range(count)])]
  transfers between devices with their start and end apart: 15 -> 17, of which waited for: 14 -> 10; matrix products, arithmetic and copies ran while one was open for 3% -> 7% of each run, Pallas kernels for 0% -> 15%
where the time goes in v2:
time: 120 us; the launch traced here: 119 us
  starting transfers between devices  43.1 us (36%)
  Pallas kernels  35.7 us (30%)
  waiting for transfers between devices  25.5 us (21%)
  other arithmetic  10.2 us (8%)
  local copies, waits for them, and re-layouts  3.32 us (3%)
  between operations  1.38 us (1%)
    pallas_call x2, Pallas kernels, windows(): pl.pallas_call(window_kernel, grid=(width_y // WIN,), in_specs=[pl.BlockS...  35.7 us
    ppermute x11, starting transfers between devices, swapped(): return lax.ppermute(value, axis, [(a, a ^ bit) for a in range(count)])  27.1 us
    ppermute x11, waiting for transfers between devices, swapped(): return lax.ppermute(value, axis, [(a, a ^ bit) for a in range(count)])  25.4 us
    ppermute x5, starting transfers between devices, passed_back(): lax.ppermute(value, axes, [(a, (a - 1) % count) for a in range(count)])  12.2 us
    ppermute x1, starting transfers between devices, passed_back_both(): return lax.ppermute(value, first + second, pairs)  3.94 us
    concatenate x3, other arithmetic, per_device(): both = jnp.concatenate([upstream, tokens], axis=3)  3.44 us
    concatenate x2, other arithmetic, per_device(): both = jnp.concatenate([both[:, SHIFT:], came_y], axis=1)  2.51 us
  transfers between devices with their start and end apart: 17, of which 10 were waited for; matrix products, arithmetic and copies ran while one was open for 7% of the time, Pallas kernels for 15%

profile of v2, /device:TPU:1, one launch (start us, length us, event | category | flops | bytes accessed | tf_op | source)
XLA Modules:
  0.0 119.2 jit_solution(17343029410516438347)
XLA Ops:
  0.6 0.0 copy-start.2
  0.7 2.1 %fusion.2 = bf16[8,4,16,384]{3,2,1,0:T(8,128)(2,1)} fusion(bf16[8,16,16,192]{3,2,1,0:T(8,128)(2,1)} %param.8, bf16[8,16,16,192]{3,2,1,0:T(8,128)(2,1)} %param.7), kind=kLoop, calls=%fused_computation.18 | loop fusion | flops 786432 | bytes 1966080 | tf_op jit(solution)/shard_map/concatenate | solution.py:269
  2.7 3.2 %collective-permute-start = (bf16[8,4,16,384]{3,2,1,0:T(8,128)(2,1)}, bf16[8,4,16,384]{3,2,1,0:T(8,128)(2,1)}, u32[]{:S(2)}, u32[]{:S(2)}) collective-permute-start(bf16[8,4,16,384]{3,2,1,0:T(8,128)(2,1)} %fusion.2), channel_id=1, source_target_pairs={{0,8},{8,0},{1,9},{9,1},{2,10},{10,2},{3,11},{11,3},{4,12},{12,4},... | collective-permute-start | bytes 1179656 | tf_op jit(solution)/shard_map/ppermute | solution.py:253
  6.0 0.9 pad_maximum_fusion.1
  6.9 4.8 %collective-permute-start.1 = (bf16[4,12,8,384]{3,2,1,0:T(8,128)(2,1)}, bf16[4,12,8,384]{3,2,1,0:T(8,128)(2,1)}, u32[]{:S(2)}, u32[]{:S(2)}) collective-permute-start(bf16[4,12,8,384]{3,2,1,0:T(8,128)(2,1)} %pad_maximum_fusion.1), channel_id=1, source_target_pairs={{0,240},{16,0},{32,16},{48,32},{64,48},{80,64},{96,80},{112,96},{1... | collective-permute-start | bytes 884744 | tf_op jit(solution)/shard_map/ppermute | solution.py:253
  11.7 0.1 pad_add_fusion.2.flags
  11.8 0.5 fusion
  12.2 0.1 pad_add_fusion.flags
  12.3 0.1 copy-done.6
  12.4 0.1 copy.16.gain
  12.6 0.1 copy.17.nbias
  12.7 0.1 reshape.317.qbias
  12.8 0.0 copy-done
  12.9 0.2 copy.15
  13.0 0.0 collective-permute-done
  13.0 1.0 slice.286
  14.0 0.6 collective-permute-start.2
  14.6 1.4 %fusion.5 = (bf16[4,16,4,384]{3,2,1,0:T(4,128)(2,1)S(1)}, bf16[4,16,4,384]{3,2,1,0:T(4,128)(2,1)S(1)}, bf16[4,16,4,384]{3,2,1,0:T(4,128)(2,1)S(1)}, bf16[4,16,4,384]{3,2,1,0:T(4,128)(2,1)S(1)}) fusion(bf16[8,12,16,384]{3,2,1,0:T(8,128)(2,1)S(1)} %fusion, bf16[8,4,16,384]{3,2,1,0:T(8,128)(2,1)} %collective-permute-done), kind=kLoop, calls=%fused_computation.25 | loop fusion | flops 1572864 | bytes 2359296 | tf_op jit(solution)/shard_map/concatenate | solution.py:274
  16.1 0.3 collective-permute-start.3
  16.4 3.9 %collective-permute-start.5 = (bf16[4,16,4,384]{3,2,1,0:T(4,128)(2,1)S(1)}, bf16[4,16,4,384]{3,2,1,0:T(4,128)(2,1)S(1)}, u32[]{:S(2)}, u32[]{:S(2)}) collective-permute-start(bf16[4,16,4,384]{3,2,1,0:T(4,128)(2,1)S(1)} %get-tuple-element.17), channel_id=1, source_target_pairs={{0,247},{1,240},{2,241},{3,242},{4,243},{5,244},{6,245},{7,246},{1... | collective-permute-start | bytes 589832 | tf_op jit(solution)/shard_map/ppermute | solution.py:263
  20.3 3.2 %collective-permute-start.4 = (bf16[4,16,4,384]{3,2,1,0:T(4,128)(2,1)S(1)}, bf16[4,16,4,384]{3,2,1,0:T(4,128)(2,1)S(1)}, u32[]{:S(2)}, u32[]{:S(2)}) collective-permute-start(bf16[4,16,4,384]{3,2,1,0:T(4,128)(2,1)S(1)} %get-tuple-element.18), channel_id=1, source_target_pairs={{0,7},{1,0},{2,1},{3,2},{4,3},{5,4},{6,5},{7,6},{8,15},{9,8},{10,9... | collective-permute-start | bytes 589832 | tf_op jit(solution)/shard_map/ppermute | solution.py:253
  23.5 1.1 fusion.1
  24.6 0.0 copy-start.1
  24.6 0.0 collective-permute-done.1
  24.6 0.0 collective-permute-done.2
  24.6 1.1 maximum_maximum_fusion.both
  25.7 17.7 %window_grads.2 = (bf16[8,16,8,192]{3,2,1,0:T(8,128)(2,1)S(1)}, f32[8,152,128]{2,1,0:T(8,128)S(1)}) custom-call(s32[3]{0:T(128)S(1)} %pad_add_fusion.flags, bf16[8,16,8,384]{3,2,1,0:T(8,128)(2,1)S(1)} %maximum_maximum_fusion.both, f32[192,1]{1,0:T(8,128)S(1)} %copy.16.gain, f32[192,1]{1,0:T(8,128)S(1)} %copy.17.nbias, bf16[576,192]{1,0:T(8,128)(2,1)S(1)} %bitcast.8, ...), custom_call_target="tpu_custom_call" | custom-call | flops 20000000000 | bytes 4000000 | tf_op jit(solution)/shard_map/window_grads/pallas_call | solution.py:161
  43.5 0.0 collective-permute-done.3
  43.5 0.0 collective-permute-done.5
  43.5 0.0 collective-permute-done.4
  43.5 0.4 maximum_maximum_fusion.1.both
  43.9 18.0 %window_grads.3 = (bf16[8,16,8,192]{3,2,1,0:T(8,128)(2,1)S(1)}, f32[8,152,128]{2,1,0:T(8,128)S(1)}) custom-call(s32[3]{0:T(128)S(1)} %pad_add_fusion.2.flags, bf16[8,16,8,384]{3,2,1,0:T(8,128)(2,1)S(1)} %maximum_maximum_fusion.1.both, f32[192,1]{1,0:T(8,128)S(1)} %copy.16.gain, f32[192,1]{1,0:T(8,128)S(1)} %copy.17.nbias, bf16[576,192]{1,0:T(8,128)(2,1)S(1)} %bitcast.9, ...), custom_call_target="tpu_custom_call" | custom-call | flops 20000000000 | bytes 4000000 | tf_op jit(solution)/shard_map/window_grads/pallas_call | solution.py:161
  61.9 0.1 add.100
  62.1 3.9 %collective-permute-start.6 = (bf16[4,160,128]{2,1,0:T(8,128)(2,1)S(1)}, bf16[4,160,128]{2,1,0:T(8,128)(2,1)S(1)}, u32[]{:S(2)}, u32[]{:S(2)}) collective-permute-start(bf16[4,160,128]{2,1,0:T(8,128)(2,1)S(1)} %pad_maximum_fusion.4), channel_id=1, source_target_pairs={{0,8},{8,0},{1,9},{9,1},{2,10},{10,2},{3,11},{11,3},{4,12},{12,4},... | collective-permute-start | bytes 491528 | tf_op jit(solution)/shard_map/ppermute | solution.py:195
  66.0 1.0 collective-permute-done.6
  67.2 0.1 collective-permute-start.7
  67.4 3.6 %collective-permute-done.7 = bf16[2,160,128]{2,1,0:T(8,128)(2,1)S(1)} collective-permute-done((bf16[2,160,128]{2,1,0:T(8,128)(2,1)S(1)}, bf16[2,160,128]{2,1,0:T(8,128)(2,1)S(1)}, u32[]{:S(2)}, u32[]{:S(2)}) %collective-permute-start.7) | collective-permute-done | bytes 81952 | tf_op jit(solution)/shard_map/ppermute | solution.py:195
  71.1 2.5 %collective-permute-start.8 = (bf16[1,160,128]{2,1,0:T(8,128)(2,1)S(1)}, bf16[1,160,128]{2,1,0:T(8,128)(2,1)S(1)}, u32[]{:S(2)}, u32[]{:S(2)}) collective-permute-start(bf16[1,160,128]{2,1,0:T(8,128)(2,1)S(1)} %pad_maximum_fusion.6), channel_id=1, source_target_pairs={{0,2},{1,3},{2,0},{3,1},{4,6},{5,7},{6,4},{7,5},{8,10},{9,11},{10,... | collective-permute-start | bytes 122888 | tf_op jit(solution)/shard_map/ppermute | solution.py:195
  73.6 2.0 %collective-permute-done.8 = bf16[1,160,128]{2,1,0:T(8,128)(2,1)S(1)} collective-permute-done((bf16[1,160,128]{2,1,0:T(8,128)(2,1)S(1)}, bf16[1,160,128]{2,1,0:T(8,128)(2,1)S(1)}, u32[]{:S(2)}, u32[]{:S(2)}) %collective-permute-start.8) | collective-permute-done | bytes 40992 | tf_op jit(solution)/shard_map/ppermute | solution.py:195
  75.7 0.1 collective-permute-start.9
  75.8 2.8 %collective-permute-done.9 = bf16[1,160,128]{2,1,0:T(8,128)(2,1)S(1)} collective-permute-done((bf16[1,160,128]{2,1,0:T(8,128)(2,1)S(1)}, bf16[1,160,128]{2,1,0:T(8,128)(2,1)S(1)}, u32[]{:S(2)}, u32[]{:S(2)}) %collective-permute-start.9) | collective-permute-done | bytes 40992 | tf_op jit(solution)/shard_map/ppermute | solution.py:195
  78.7 3.0 %collective-permute-start.10 = (bf16[1,160,128]{2,1,0:T(8,128)(2,1)S(1)}, bf16[1,160,128]{2,1,0:T(8,128)(2,1)S(1)}, u32[]{:S(2)}, u32[]{:S(2)}) collective-permute-start(bf16[1,160,128]{2,1,0:T(8,128)(2,1)S(1)} %pad_maximum_fusion.8), channel_id=1, source_target_pairs={{0,32},{16,48},{32,0},{48,16},{1,33},{17,49},{33,1},{49,17},{2,34}... | collective-permute-start | bytes 122888 | tf_op jit(solution)/shard_map/ppermute | solution.py:195
  81.7 1.5 %collective-permute-done.10 = bf16[1,160,128]{2,1,0:T(8,128)(2,1)S(1)} collective-permute-done((bf16[1,160,128]{2,1,0:T(8,128)(2,1)S(1)}, bf16[1,160,128]{2,1,0:T(8,128)(2,1)S(1)}, u32[]{:S(2)}, u32[]{:S(2)}) %collective-permute-start.10) | collective-permute-done | bytes 40992 | tf_op jit(solution)/shard_map/ppermute | solution.py:195
  83.3 0.1 collective-permute-start.11
  83.4 3.1 %collective-permute-done.11 = bf16[1,160,128]{2,1,0:T(8,128)(2,1)S(1)} collective-permute-done((bf16[1,160,128]{2,1,0:T(8,128)(2,1)S(1)}, bf16[1,160,128]{2,1,0:T(8,128)(2,1)S(1)}, u32[]{:S(2)}, u32[]{:S(2)}) %collective-permute-start.11) | collective-permute-done | bytes 40992 | tf_op jit(solution)/shard_map/ppermute | solution.py:195
  86.6 2.4 %collective-permute-start.12 = (bf16[1,160,128]{2,1,0:T(8,128)(2,1)S(1)}, bf16[1,160,128]{2,1,0:T(8,128)(2,1)S(1)}, u32[]{:S(2)}, u32[]{:S(2)}) collective-permute-start(bf16[1,160,128]{2,1,0:T(8,128)(2,1)S(1)} %pad_maximum_fusion.10), channel_id=1, source_target_pairs={{0,128},{64,192},{128,0},{192,64},{1,129},{65,193},{129,1},{193,65... | collective-permute-start | bytes 122888 | tf_op jit(solution)/shard_map/ppermute | solution.py:195
  89.0 1.4 %collective-permute-done.12 = bf16[1,160,128]{2,1,0:T(8,128)(2,1)S(1)} collective-permute-done((bf16[1,160,128]{2,1,0:T(8,128)(2,1)S(1)}, bf16[1,160,128]{2,1,0:T(8,128)(2,1)S(1)}, u32[]{:S(2)}, u32[]{:S(2)}) %collective-permute-start.12) | collective-permute-done | bytes 40992 | tf_op jit(solution)/shard_map/ppermute | solution.py:195
  90.5 2.0 %collective-permute-start.13 = (bf16[1,160,128]{2,1,0:T(8,128)(2,1)S(1)}, bf16[1,160,128]{2,1,0:T(8,128)(2,1)S(1)}, u32[]{:S(2)}, u32[]{:S(2)}) collective-permute-start(bf16[1,160,128]{2,1,0:T(8,128)(2,1)S(1)} %pad_maximum_fusion.11), channel_id=1, source_target_pairs={{0,4},{4,0},{1,5},{5,1},{2,6},{6,2},{3,7},{7,3},{8,12},{12,8},{9,1... | collective-permute-start | bytes 122888 | tf_op jit(solution)/shard_map/ppermute | solution.py:195
  92.6 5.3 %collective-permute-done.13 = bf16[1,160,128]{2,1,0:T(8,128)(2,1)S(1)} collective-permute-done((bf16[1,160,128]{2,1,0:T(8,128)(2,1)S(1)}, bf16[1,160,128]{2,1,0:T(8,128)(2,1)S(1)}, u32[]{:S(2)}, u32[]{:S(2)}) %collective-permute-start.13) | collective-permute-done | bytes 40992 | tf_op jit(solution)/shard_map/ppermute | solution.py:195
  98.0 2.7 %collective-permute-start.14 = (bf16[1,160,128]{2,1,0:T(8,128)(2,1)S(1)}, bf16[1,160,128]{2,1,0:T(8,128)(2,1)S(1)}, u32[]{:S(2)}, u32[]{:S(2)}) collective-permute-start(bf16[1,160,128]{2,1,0:T(8,128)(2,1)S(1)} %pad_maximum_fusion.12), channel_id=1, source_target_pairs={{0,2},{1,3},{2,0},{3,1},{4,6},{5,7},{6,4},{7,5},{8,10},{9,11},{10,... | collective-permute-start | bytes 122888 | tf_op jit(solution)/shard_map/ppermute | solution.py:195
  100.7 1.7 %collective-permute-done.14 = bf16[1,160,128]{2,1,0:T(8,128)(2,1)S(1)} collective-permute-done((bf16[1,160,128]{2,1,0:T(8,128)(2,1)S(1)}, bf16[1,160,128]{2,1,0:T(8,128)(2,1)S(1)}, u32[]{:S(2)}, u32[]{:S(2)}) %collective-permute-start.14) | collective-permute-done | bytes 40992 | tf_op jit(solution)/shard_map/ppermute | solution.py:195
  102.4 0.4 collective-permute-start.15
  102.8 3.0 %collective-permute-done.15 = bf16[2,160,128]{2,1,0:T(8,128)(2,1)S(1)} collective-permute-done((bf16[2,160,128]{2,1,0:T(8,128)(2,1)S(1)}, bf16[2,160,128]{2,1,0:T(8,128)(2,1)S(1)}, u32[]{:S(2)}, u32[]{:S(2)}) %collective-permute-start.15) | collective-permute-done | bytes 81952 | tf_op jit(solution)/shard_map/ppermute | solution.py:195
  105.8 9.8 %collective-permute-start.16 = (bf16[4,160,128]{2,1,0:T(8,128)(2,1)S(1)}, bf16[4,160,128]{2,1,0:T(8,128)(2,1)S(1)}, u32[]{:S(2)}, u32[]{:S(2)}) collective-permute-start(bf16[4,160,128]{2,1,0:T(8,128)(2,1)S(1)} %maximum_select_fusion.1), channel_id=1, source_target_pairs={{0,8},{8,0},{1,9},{9,1},{2,10},{10,2},{3,11},{11,3},{4,12},{12,4},... | collective-permute-start | bytes 491528 | tf_op jit(solution)/shard_map/ppermute | solution.py:195
  115.6 1.2 pad_maximum_fusion
  116.8 0.0 collective-permute-done.16
  116.8 0.1 fusion.3
  116.9 0.1 maximum_multiply_fusion
  117.1 0.6 fusion.18
  117.6 0.6 slice.339
  118.3 0.1 fusion.17
  118.4 0.0 copy-start.4
  118.4 0.7 pad_maximum_fusion.3
  119.1 0.1 copy-done.4
  (79 shorter events, 0.8 us)
Async XLA Ops:
  0.6 5.3 %copy-start.2 = (bf16[8,16,16,192]{3,2,1,0:T(8,128)(2,1)S(1)}, bf16[8,16,16,192]{3,2,1,0:T(8,128)(2,1)}, u32[]{:S(2)}) copy-start(bf16[8,16,16,192]{3,2,1,0:T(8,128)(2,1)} %param.8) | copy-start | bytes 2359300
  0.6 5.3 %copy-start.3 = (bf16[8,16,16,192]{3,2,1,0:T(8,128)(2,1)S(1)}, bf16[8,16,16,192]{3,2,1,0:T(8,128)(2,1)}, u32[]{:S(2)}) copy-start(bf16[8,16,16,192]{3,2,1,0:T(8,128)(2,1)} %param.7) | copy-start | bytes 2359300
  2.7 10.3 %collective-permute-start = (bf16[8,4,16,384]{3,2,1,0:T(8,128)(2,1)}, bf16[8,4,16,384]{3,2,1,0:T(8,128)(2,1)}, u32[]{:S(2)}, u32[]{:S(2)}) collective-permute-start(bf16[8,4,16,384]{3,2,1,0:T(8,128)(2,1)} %fusion.2), channel_id=1, source_target_pairs={{0,8},{8,0},{1,9},{9,1},{2,10},{10,2},{3,11},{11,3},{4,12},{12,4},... | collective-permute-start | bytes 1179656 | tf_op jit(solution)/shard_map/ppermute | solution.py:253
  6.9 17.7 %collective-permute-start.1 = (bf16[4,12,8,384]{3,2,1,0:T(8,128)(2,1)}, bf16[4,12,8,384]{3,2,1,0:T(8,128)(2,1)}, u32[]{:S(2)}, u32[]{:S(2)}) collective-permute-start(bf16[4,12,8,384]{3,2,1,0:T(8,128)(2,1)} %pad_maximum_fusion.1), channel_id=1, source_target_pairs={{0,240},{16,0},{32,16},{48,32},{64,48},{80,64},{96,80},{112,96},{1... | collective-permute-start | bytes 884744 | tf_op jit(solution)/shard_map/ppermute | solution.py:253
  11.8 0.7 copy-start.6
  11.8 0.8 copy-start.7
  11.8 0.9 copy-start.5
  11.8 1.1 copy-start
  14.0 10.6 %collective-permute-start.2 = (bf16[4,4,8,384]{3,2,1,0:T(8,128)(2,1)S(1)}, bf16[4,4,8,384]{3,2,1,0:T(8,128)(2,1)S(1)}, u32[]{:S(2)}, u32[]{:S(2)}) collective-permute-start(bf16[4,4,8,384]{3,2,1,0:T(8,128)(2,1)S(1)} %slice.286), channel_id=1, source_target_pairs={{0,240},{16,0},{32,16},{48,32},{64,48},{80,64},{96,80},{112,96},{1... | collective-permute-start | bytes 294920 | tf_op jit(solution)/shard_map/ppermute | solution.py:253
  16.1 27.4 %collective-permute-start.3 = (bf16[4,16,4,384]{3,2,1,0:T(4,128)(2,1)S(1)}, bf16[4,16,4,384]{3,2,1,0:T(4,128)(2,1)S(1)}, u32[]{:S(2)}, u32[]{:S(2)}) collective-permute-start(bf16[4,16,4,384]{3,2,1,0:T(4,128)(2,1)S(1)} %get-tuple-element.16), channel_id=1, source_target_pairs={{0,240},{16,0},{32,16},{48,32},{64,48},{80,64},{96,80},{112,96},{1... | collective-permute-start | bytes 589832 | tf_op jit(solution)/shard_map/ppermute | solution.py:253
  16.4 27.1 %collective-permute-start.5 = (bf16[4,16,4,384]{3,2,1,0:T(4,128)(2,1)S(1)}, bf16[4,16,4,384]{3,2,1,0:T(4,128)(2,1)S(1)}, u32[]{:S(2)}, u32[]{:S(2)}) collective-permute-start(bf16[4,16,4,384]{3,2,1,0:T(4,128)(2,1)S(1)} %get-tuple-element.17), channel_id=1, source_target_pairs={{0,247},{1,240},{2,241},{3,242},{4,243},{5,244},{6,245},{7,246},{1... | collective-permute-start | bytes 589832 | tf_op jit(solution)/shard_map/ppermute | solution.py:263
  20.3 23.2 %collective-permute-start.4 = (bf16[4,16,4,384]{3,2,1,0:T(4,128)(2,1)S(1)}, bf16[4,16,4,384]{3,2,1,0:T(4,128)(2,1)S(1)}, u32[]{:S(2)}, u32[]{:S(2)}) collective-permute-start(bf16[4,16,4,384]{3,2,1,0:T(4,128)(2,1)S(1)} %get-tuple-element.18), channel_id=1, source_target_pairs={{0,7},{1,0},{2,1},{3,2},{4,3},{5,4},{6,5},{7,6},{8,15},{9,8},{10,9... | collective-permute-start | bytes 589832 | tf_op jit(solution)/shard_map/ppermute | solution.py:253
  24.6 1.1 copy-start.1
  62.1 5.0 %collective-permute-start.6 = (bf16[4,160,128]{2,1,0:T(8,128)(2,1)S(1)}, bf16[4,160,128]{2,1,0:T(8,128)(2,1)S(1)}, u32[]{:S(2)}, u32[]{:S(2)}) collective-permute-start(bf16[4,160,128]{2,1,0:T(8,128)(2,1)S(1)} %pad_maximum_fusion.4), channel_id=1, source_target_pairs={{0,8},{8,0},{1,9},{9,1},{2,10},{10,2},{3,11},{11,3},{4,12},{12,4},... | collective-permute-start | bytes 491528 | tf_op jit(solution)/shard_map/ppermute | solution.py:195
  67.2 3.8 %collective-permute-start.7 = (bf16[2,160,128]{2,1,0:T(8,128)(2,1)S(1)}, bf16[2,160,128]{2,1,0:T(8,128)(2,1)S(1)}, u32[]{:S(2)}, u32[]{:S(2)}) collective-permute-start(bf16[2,160,128]{2,1,0:T(8,128)(2,1)S(1)} %pad_maximum_fusion.5), channel_id=1, source_target_pairs={{0,1},{1,0},{2,3},{3,2},{4,5},{5,4},{6,7},{7,6},{8,9},{9,8},{10,11... | collective-permute-start | bytes 245768 | tf_op jit(solution)/shard_map/ppermute | solution.py:195
  71.1 4.4 %collective-permute-start.8 = (bf16[1,160,128]{2,1,0:T(8,128)(2,1)S(1)}, bf16[1,160,128]{2,1,0:T(8,128)(2,1)S(1)}, u32[]{:S(2)}, u32[]{:S(2)}) collective-permute-start(bf16[1,160,128]{2,1,0:T(8,128)(2,1)S(1)} %pad_maximum_fusion.6), channel_id=1, source_target_pairs={{0,2},{1,3},{2,0},{3,1},{4,6},{5,7},{6,4},{7,5},{8,10},{9,11},{10,... | collective-permute-start | bytes 122888 | tf_op jit(solution)/shard_map/ppermute | solution.py:195
  75.7 2.9 %collective-permute-start.9 = (bf16[1,160,128]{2,1,0:T(8,128)(2,1)S(1)}, bf16[1,160,128]{2,1,0:T(8,128)(2,1)S(1)}, u32[]{:S(2)}, u32[]{:S(2)}) collective-permute-start(bf16[1,160,128]{2,1,0:T(8,128)(2,1)S(1)} %pad_maximum_fusion.7), channel_id=1, source_target_pairs={{0,16},{16,0},{32,48},{48,32},{1,17},{17,1},{33,49},{49,33},{2,18}... | collective-permute-start | bytes 122888 | tf_op jit(solution)/shard_map/ppermute | solution.py:195
  78.7 4.4 %collective-permute-start.10 = (bf16[1,160,128]{2,1,0:T(8,128)(2,1)S(1)}, bf16[1,160,128]{2,1,0:T(8,128)(2,1)S(1)}, u32[]{:S(2)}, u32[]{:S(2)}) collective-permute-start(bf16[1,160,128]{2,1,0:T(8,128)(2,1)S(1)} %pad_maximum_fusion.8), channel_id=1, source_target_pairs={{0,32},{16,48},{32,0},{48,16},{1,33},{17,49},{33,1},{49,17},{2,34}... | collective-permute-start | bytes 122888 | tf_op jit(solution)/shard_map/ppermute | solution.py:195
  83.3 3.2 %collective-permute-start.11 = (bf16[1,160,128]{2,1,0:T(8,128)(2,1)S(1)}, bf16[1,160,128]{2,1,0:T(8,128)(2,1)S(1)}, u32[]{:S(2)}, u32[]{:S(2)}) collective-permute-start(bf16[1,160,128]{2,1,0:T(8,128)(2,1)S(1)} %pad_maximum_fusion.9), channel_id=1, source_target_pairs={{0,64},{64,0},{128,192},{192,128},{1,65},{65,1},{129,193},{193,129... | collective-permute-start | bytes 122888 | tf_op jit(solution)/shard_map/ppermute | solution.py:195
  86.6 3.8 %collective-permute-start.12 = (bf16[1,160,128]{2,1,0:T(8,128)(2,1)S(1)}, bf16[1,160,128]{2,1,0:T(8,128)(2,1)S(1)}, u32[]{:S(2)}, u32[]{:S(2)}) collective-permute-start(bf16[1,160,128]{2,1,0:T(8,128)(2,1)S(1)} %pad_maximum_fusion.10), channel_id=1, source_target_pairs={{0,128},{64,192},{128,0},{192,64},{1,129},{65,193},{129,1},{193,65... | collective-permute-start | bytes 122888 | tf_op jit(solution)/shard_map/ppermute | solution.py:195
  90.5 7.3 %collective-permute-start.13 = (bf16[1,160,128]{2,1,0:T(8,128)(2,1)S(1)}, bf16[1,160,128]{2,1,0:T(8,128)(2,1)S(1)}, u32[]{:S(2)}, u32[]{:S(2)}) collective-permute-start(bf16[1,160,128]{2,1,0:T(8,128)(2,1)S(1)} %pad_maximum_fusion.11), channel_id=1, source_target_pairs={{0,4},{4,0},{1,5},{5,1},{2,6},{6,2},{3,7},{7,3},{8,12},{12,8},{9,1... | collective-permute-start | bytes 122888 | tf_op jit(solution)/shard_map/ppermute | solution.py:195
  98.0 4.4 %collective-permute-start.14 = (bf16[1,160,128]{2,1,0:T(8,128)(2,1)S(1)}, bf16[1,160,128]{2,1,0:T(8,128)(2,1)S(1)}, u32[]{:S(2)}, u32[]{:S(2)}) collective-permute-start(bf16[1,160,128]{2,1,0:T(8,128)(2,1)S(1)} %pad_maximum_fusion.12), channel_id=1, source_target_pairs={{0,2},{1,3},{2,0},{3,1},{4,6},{5,7},{6,4},{7,5},{8,10},{9,11},{10,... | collective-permute-start | bytes 122888 | tf_op jit(solution)/shard_map/ppermute | solution.py:195
  102.4 3.4 %collective-permute-start.15 = (bf16[2,160,128]{2,1,0:T(8,128)(2,1)S(1)}, bf16[2,160,128]{2,1,0:T(8,128)(2,1)S(1)}, u32[]{:S(2)}, u32[]{:S(2)}) collective-permute-start(bf16[2,160,128]{2,1,0:T(8,128)(2,1)S(1)} %maximum_select_fusion.2), channel_id=1, source_target_pairs={{0,1},{1,0},{2,3},{3,2},{4,5},{5,4},{6,7},{7,6},{8,9},{9,8},{10,11... | collective-permute-start | bytes 245768 | tf_op jit(solution)/shard_map/ppermute | solution.py:195
  105.8 11.0 %collective-permute-start.16 = (bf16[4,160,128]{2,1,0:T(8,128)(2,1)S(1)}, bf16[4,160,128]{2,1,0:T(8,128)(2,1)S(1)}, u32[]{:S(2)}, u32[]{:S(2)}) collective-permute-start(bf16[4,160,128]{2,1,0:T(8,128)(2,1)S(1)} %maximum_select_fusion.1), channel_id=1, source_target_pairs={{0,8},{8,0},{1,9},{9,1},{2,10},{10,2},{3,11},{11,3},{4,12},{12,4},... | collective-permute-start | bytes 491528 | tf_op jit(solution)/shard_map/ppermute | solution.py:195
  118.4 0.8 copy-start.4

commit v3 on v2

--- a/solution.py
+++ b/solution.py
@@ -75,34 +75,49 @@
     key_code = jnp.where(same, 0.0, FAR).astype(BF16)
     ones = jnp.ones((16, count), BF16)
 
-    for head in range(HEADS):
-        lo = size * head
-        at_q = slice(lo, lo + size)
-        at_k = slice(width + lo, width + lo + size)
-        at_v = slice(2 * width + lo, 2 * width + lo + size)
-        query, keyset, valset, grad = packed[at_q], packed[at_k], packed[at_v], att_grad[at_q]
-        value_ones = jnp.concatenate([valset, ones], axis=0)
-        scores = dot_cols(
-            jnp.concatenate([keyset, key_code], axis=0),
-            jnp.concatenate([query, query_code], axis=0),
+    def rows_of(kind, head):
+        return slice(kind * width + size * head, kind * width + size * (head + 1))
+
+    def score(head):
+        return dot_cols(
+            jnp.concatenate([packed[rows_of(1, head)], key_code], axis=0),
+            jnp.concatenate([packed[rows_of(0, head)], query_code], axis=0),
         )
+
+    def weigh(scores):
         peak = jnp.max(scores, axis=0, keepdims=True)
-        expo = jnp.exp2(scores * scale - peak * scale).astype(BF16)
-        mixed = dot(value_ones, expo)
+        return jnp.exp2((scores - peak) * scale).astype(BF16)
+
+    def values(head):
+        return jnp.concatenate([packed[rows_of(2, head)], ones], axis=0)
+
+    def attend(head, expo):
+        mixed = dot(values(head), expo)
         recip = 1.0 / mixed[size : size + 1]
         result = mixed[:size] * recip
-        attended[at_q, :] = result.astype(BF16)
-        grad_scaled = (grad.astype(F32) * recip).astype(BF16)
-        inner = jnp.sum(grad_scaled.astype(F32) * result, axis=0, keepdims=True)
-        inner_high = inner.astype(BF16).astype(F32)
-        inner_rows = jnp.where(
-            row == 0, -inner_high, jnp.where(row == 1, inner_high - inner, 0.0)
-        ).astype(BF16)
-        spread = dot_cols(value_ones, jnp.concatenate([grad_scaled, inner_rows], axis=0))
+        attended[rows_of(0, head), :] = result.astype(BF16)
+        scaled = (att_grad[rows_of(0, head)].astype(F32) * recip).astype(BF16)
+        inner = jnp.sum(scaled.astype(F32) * result, axis=0, keepdims=True)
+        high = inner.astype(BF16).astype(F32)
+        inner_rows = jnp.where(row == 0, -high, jnp.where(row == 1, high - inner, 0.0))
+        return scaled, jnp.concatenate([scaled, inner_rows.astype(BF16)], axis=0)
+
+    def pull_back(head, expo, scaled, spread):
         score_grad = expo * spread.astype(BF16)
-        packed_grad[at_q, :] = (dot(keyset, score_grad) * factor).astype(BF16)
-        packed_grad[at_k, :] = (dot_rows(query, score_grad) * factor).astype(BF16)
-        packed_grad[at_v, :] = dot_rows(grad_scaled, expo).astype(BF16)
+        query, keyset = packed[rows_of(0, head)], packed[rows_of(1, head)]
+        packed_grad[rows_of(2, head), :] = dot_rows(expo, scaled).T.astype(BF16)
+        packed_grad[rows_of(0, head), :] = (dot(keyset, score_grad) * factor).astype(BF16)
+        packed_grad[rows_of(1, head), :] = (dot_rows(score_grad, query).T * factor).astype(BF16)
+
+    scores, earlier = score(0), None
+    for head in range(HEADS + 1):
+        following = score(head + 1) if head + 1 < HEADS else None
+        expo = weigh(scores) if head < HEADS else None
+        spread = None if earlier is None else dot_cols(values(head - 1), earlier[2])
+        current = (expo, *attend(head, expo)) if head < HEADS else None
+        if earlier is not None:
+            pull_back(head - 1, earlier[0], earlier[1], spread)
+        scores, earlier = following, current
 
     grad_half = packed_grad[...]
     acc_qkv[...] += dot_rows(jnp.concatenate([hidden, ones], axis=0), grad_half)
@@ -191,7 +206,8 @@
 
 
 def swapped(value, axis, bit):
-    count = lax.axis_size(axis)
+    axes = (axis,) if isinstance(axis, str) else axis
+    count = math.prod(lax.axis_size(name) for name in axes)
     return lax.ppermute(value, axis, [(a, a ^ bit) for a in range(count)])
 
 
@@ -207,44 +223,64 @@
     return jnp.concatenate([wide[:, :MAIN], small], axis=1)
 
 
-def exchanged(value, axis, bit):
-    return decoded(swapped(coded(value), axis, bit))
-
-
-def halve(value, axis, bit):
+def halve(value, axis):
     half = value.shape[0] // 2
-    upper = (lax.axis_index(axis) // bit) % 2
+    upper = lax.axis_index(axis) % 2
     kept = lax.dynamic_slice_in_dim(value, upper * half, half, 0)
     given = lax.dynamic_slice_in_dim(value, (1 - upper) * half, half, 0)
-    return kept + exchanged(given, axis, bit)
-
-
-def join(value, axis, bit):
-    upper = (lax.axis_index(axis) // bit) % 2
-    other = swapped(value, axis, bit)
-    return jnp.where(
-        upper == 0,
-        jnp.concatenate([value, other], axis=0),
-        jnp.concatenate([other, value], axis=0),
-    )
-
-
-def bits_of(axis):
-    return [1 << j for j in range(lax.axis_size(axis).bit_length() - 1)]
+    return kept + decoded(swapped(coded(given), axis, 1))
+
+
+def quarter(value, axis):
+    part = value.shape[0] // 4
+    at = lax.axis_index(axis)
+    sent = coded(value)
+    total = lax.dynamic_slice_in_dim(value, at * part, part, 0)
+    for bits in (2, 1, 3):
+        given = lax.dynamic_slice_in_dim(sent, (at ^ bits) * part, part, 0)
+        total = total + decoded(swapped(given, axis, bits))
+    return total
+
+
+def sum_of_two(value, axes, bit):
+    sent = coded(value)
+    return decoded(sent) + decoded(swapped(sent, axes, bit))
+
+
+def sum_of_four(value, axes, first, second):
+    sent = coded(value)
+    both = swapped(sent, axes, first ^ second)
+    one, two = swapped(sent, axes, first), swapped(sent, axes, second)
+    return (decoded(sent) + decoded(one)) + (decoded(two) + decoded(both))
+
+
+def join(value, axis):
+    upper = lax.axis_index(axis) % 2 == 1
+    other = swapped(value, axis, 1)
+    return jnp.concatenate(
+        [jnp.where(upper, other, value), jnp.where(upper, value, other)], axis=0
+    )
+
+
+def join_four(value, axis):
+    at = lax.axis_index(axis)
+    odd, upper = at % 2 == 1, at >= 2
+    far, one, three = (swapped(value, axis, bits) for bits in (2, 1, 3))
+    flat = [
+        jnp.where(odd, one, value),
+        jnp.where(odd, value, one),
+        jnp.where(odd, three, far),
+        jnp.where(odd, far, three),
+    ]
+    return jnp.concatenate([jnp.where(upper, flat[j ^ 2], flat[j]) for j in range(4)], axis=0)
 
 
 def summed_everywhere(value):
-    for axis in ("c", "y"):
-        for bit in bits_of(axis):
-            value = halve(value, axis, bit)
-    for axis in ("x", "zl", "zh"):
-        for bit in bits_of(axis):
-            value = value + exchanged(value, axis, bit)
-    value = coded(value)
-    for axis in ("y", "c"):
-        for bit in reversed(bits_of(axis)):
-            value = join(value, axis, bit)
-    return decoded(value)
+    value = quarter(halve(value, "c"), "y")
+    value = sum_of_four(value, ("x",), 1, 2)
+    value = sum_of_two(value, ("zl", "zh"), 2)
+    value = sum_of_four(value, ("zl", "zh"), 4, 1)
+    return decoded(join(join_four(coded(value), "y"), "c"))
 
 
 def passed_back(value, axes):

time: 120 us -> 106 us (0.88)
  Pallas kernels: 35.7 us -> 26.6 us
  waiting for transfers between devices: 25.5 us -> 19.4 us
  starting transfers between devices: 43.1 us -> 45.1 us
    ppermute x11 -> x15, waiting for transfers between devices: 25.4 us -> 15.6 us  [swapped(): return lax.ppermute(value, axis, [(a, a ^ bit) for a in range(count)])]
    pallas_call x2, Pallas kernels: 35.7 us -> 26.6 us  [windows(): pl.pallas_call(window_kernel, grid=(width_y // WIN,), in_specs=[pl.BlockS...]
    ppermute x5, waiting for transfers between devices: 0.01 us -> 3.82 us  [passed_back(): lax.ppermute(value, axes, [(a, (a - 1) % count) for a in range(count)])]
    ppermute x11 -> x15, starting transfers between devices: 27.1 us -> 29 us  [swapped(): return lax.ppermute(value, axis, [(a, a ^ bit) for a in range(count)])]
  transfers between devices with their start and end apart: 17 -> 21, of which waited for: 10 -> 10; matrix products, arithmetic and copies ran while one was open for 7% -> 7% of each run, Pallas kernels for 15% -> 12%
where the time goes in v3:
time: 106 us
  starting transfers between devices  45.1 us (43%)
  Pallas kernels  26.6 us (25%)
  waiting for transfers between devices  19.4 us (18%)
  other arithmetic  10.3 us (10%)
  local copies, waits for them, and re-layouts  3.34 us (3%)
  between operations  1.4 us (1%)
    ppermute x15, starting transfers between devices, swapped(): return lax.ppermute(value, axis, [(a, a ^ bit) for a in range(count)])  29 us
    pallas_call x2, Pallas kernels, windows(): pl.pallas_call(window_kernel, grid=(width_y // WIN,), in_specs=[pl.BlockS...  26.6 us
    ppermute x15, waiting for transfers between devices, swapped(): return lax.ppermute(value, axis, [(a, a ^ bit) for a in range(count)])  15.6 us
    ppermute x5, starting transfers between devices, passed_back(): lax.ppermute(value, axes, [(a, (a - 1) % count) for a in range(count)])  12.2 us
    ppermute x1, starting transfers between devices, passed_back_both(): return lax.ppermute(value, first + second, pairs)  3.94 us
    ppermute x5, waiting for transfers between devices, passed_back(): lax.ppermute(value, axes, [(a, (a - 1) % count) for a in range(count)])  3.82 us
    concatenate x3, other arithmetic, per_device(): both = jnp.concatenate([upstream, tokens], axis=3)  3.44 us
    concatenate x2, other arithmetic, per_device(): both = jnp.concatenate([both[:, SHIFT:], came_y], axis=1)  2.51 us
  transfers between devices with their start and end apart: 21, of which 10 were waited for; matrix products, arithmetic and copies ran while one was open for 7% of the time, Pallas kernels for 12%

profile of v3, /device:TPU:1, one launch (start us, length us, event | category | flops | bytes accessed | tf_op | source)
XLA Modules:
  0.0 106.2 jit_solution(12342587588650623985)
XLA Ops:
  0.7 2.1 %fusion.2 = bf16[8,4,16,384]{3,2,1,0:T(8,128)(2,1)} fusion(bf16[8,16,16,192]{3,2,1,0:T(8,128)(2,1)} %param.8, bf16[8,16,16,192]{3,2,1,0:T(8,128)(2,1)} %param.7), kind=kLoop, calls=%fused_computation.18 | loop fusion | flops 786432 | bytes 1966080 | tf_op jit(solution)/shard_map/concatenate | solution.py:305
  2.7 3.2 %collective-permute-start = (bf16[8,4,16,384]{3,2,1,0:T(8,128)(2,1)}, bf16[8,4,16,384]{3,2,1,0:T(8,128)(2,1)}, u32[]{:S(2)}, u32[]{:S(2)}) collective-permute-start(bf16[8,4,16,384]{3,2,1,0:T(8,128)(2,1)} %fusion.2), channel_id=1, source_target_pairs={{0,8},{8,0},{1,9},{9,1},{2,10},{10,2},{3,11},{11,3},{4,12},{12,4},... | collective-permute-start | bytes 1179656 | tf_op jit(solution)/shard_map/ppermute | solution.py:289
  6.0 0.9 pad_maximum_fusion.1
  6.9 4.8 %collective-permute-start.1 = (bf16[4,12,8,384]{3,2,1,0:T(8,128)(2,1)}, bf16[4,12,8,384]{3,2,1,0:T(8,128)(2,1)}, u32[]{:S(2)}, u32[]{:S(2)}) collective-permute-start(bf16[4,12,8,384]{3,2,1,0:T(8,128)(2,1)} %pad_maximum_fusion.1), channel_id=1, source_target_pairs={{0,240},{16,0},{32,16},{48,32},{64,48},{80,64},{96,80},{112,96},{1... | collective-permute-start | bytes 884744 | tf_op jit(solution)/shard_map/ppermute | solution.py:289
  11.7 0.1 pad_add_fusion.2.flags
  11.8 0.5 fusion
  12.2 0.1 pad_add_fusion.flags
  12.3 0.1 copy-done.6
  12.4 0.1 copy.16.gain
  12.6 0.1 copy.17.nbias
  12.7 0.1 reshape.549.qbias
  12.9 0.2 copy.15
  13.0 0.0 collective-permute-done
  13.0 1.0 slice.331
  14.0 0.6 collective-permute-start.2
  14.6 1.4 %fusion.4 = (bf16[4,16,4,384]{3,2,1,0:T(4,128)(2,1)S(1)}, bf16[4,16,4,384]{3,2,1,0:T(4,128)(2,1)S(1)}, bf16[4,16,4,384]{3,2,1,0:T(4,128)(2,1)S(1)}, bf16[4,16,4,384]{3,2,1,0:T(4,128)(2,1)S(1)}) fusion(bf16[8,12,16,384]{3,2,1,0:T(8,128)(2,1)S(1)} %fusion, bf16[8,4,16,384]{3,2,1,0:T(8,128)(2,1)} %collective-permute-done), kind=kLoop, calls=%fused_computation.25 | loop fusion | flops 1572864 | bytes 2359296 | tf_op jit(solution)/shard_map/concatenate | solution.py:310
  16.1 0.3 collective-permute-start.3
  16.4 3.9 %collective-permute-start.5 = (bf16[4,16,4,384]{3,2,1,0:T(4,128)(2,1)S(1)}, bf16[4,16,4,384]{3,2,1,0:T(4,128)(2,1)S(1)}, u32[]{:S(2)}, u32[]{:S(2)}) collective-permute-start(bf16[4,16,4,384]{3,2,1,0:T(4,128)(2,1)S(1)} %get-tuple-element.23), channel_id=1, source_target_pairs={{0,247},{1,240},{2,241},{3,242},{4,243},{5,244},{6,245},{7,246},{1... | collective-permute-start | bytes 589832 | tf_op jit(solution)/shard_map/ppermute | solution.py:299
  20.3 3.2 %collective-permute-start.4 = (bf16[4,16,4,384]{3,2,1,0:T(4,128)(2,1)S(1)}, bf16[4,16,4,384]{3,2,1,0:T(4,128)(2,1)S(1)}, u32[]{:S(2)}, u32[]{:S(2)}) collective-permute-start(bf16[4,16,4,384]{3,2,1,0:T(4,128)(2,1)S(1)} %get-tuple-element.24), channel_id=1, source_target_pairs={{0,7},{1,0},{2,1},{3,2},{4,3},{5,4},{6,5},{7,6},{8,15},{9,8},{10,9... | collective-permute-start | bytes 589832 | tf_op jit(solution)/shard_map/ppermute | solution.py:289
  23.5 1.1 %fusion.1 = bf16[4,16,8,384]{3,2,1,0:T(8,128)(2,1)S(1)} fusion(bf16[8,12,16,384]{3,2,1,0:T(8,128)(2,1)S(1)} %fusion, bf16[8,4,16,384]{3,2,1,0:T(8,128)(2,1)} %collective-permute-done), kind=kLoop, calls=%fused_computation.17 | loop fusion | flops 196608 | bytes 1966080 | tf_op jit(solution)/shard_map/concatenate | solution.py:310
  24.6 0.0 copy-start.1
  24.6 0.0 collective-permute-done.1
  24.6 1.1 %maximum_maximum_fusion.both = bf16[8,16,8,384]{3,2,1,0:T(8,128)(2,1)S(1)} fusion(bf16[4,4,8,384]{3,2,1,0:T(8,128)(2,1)S(1)} %collective-permute-done.2, bf16[4,12,8,384]{3,2,1,0:T(8,128)(2,1)} %collective-permute-done.1, bf16[4,16,8,384]{3,2,1,0:T(8,128)(2,1)S(1)} %fusion.1), kind=kLoop, calls=%fused_computation.14 | loop fusion | flops 786432 | bytes 1572864 | tf_op jit(solution)/shard_map/concatenate | solution.py:315
  25.7 13.2 %window_grads.2 = (bf16[8,16,8,192]{3,2,1,0:T(8,128)(2,1)S(1)}, f32[8,152,128]{2,1,0:T(8,128)S(1)}) custom-call(s32[3]{0:T(128)S(1)} %pad_add_fusion.flags, bf16[8,16,8,384]{3,2,1,0:T(8,128)(2,1)S(1)} %maximum_maximum_fusion.both, f32[192,1]{1,0:T(8,128)S(1)} %copy.16.gain, f32[192,1]{1,0:T(8,128)S(1)} %copy.17.nbias, bf16[576,192]{1,0:T(8,128)(2,1)S(1)} %bitcast.8, ...), custom_call_target="tpu_custom_call" | custom-call | flops 20000000000 | bytes 4000000 | tf_op jit(solution)/shard_map/window_grads/pallas_call | solution.py:176
  38.9 0.0 collective-permute-done.3
  39.0 3.8 %collective-permute-done.4 = bf16[4,16,4,384]{3,2,1,0:T(4,128)(2,1)S(1)} collective-permute-done((bf16[4,16,4,384]{3,2,1,0:T(4,128)(2,1)S(1)}, bf16[4,16,4,384]{3,2,1,0:T(4,128)(2,1)S(1)}, u32[]{:S(2)}, u32[]{:S(2)}) %collective-permute-start.4) | collective-permute-done | bytes 196640 | tf_op jit(solution)/shard_map/ppermute | solution.py:289
  42.8 0.4 maximum_maximum_fusion.1.both
  43.2 13.4 %window_grads.3 = (bf16[8,16,8,192]{3,2,1,0:T(8,128)(2,1)S(1)}, f32[8,152,128]{2,1,0:T(8,128)S(1)}) custom-call(s32[3]{0:T(128)S(1)} %pad_add_fusion.2.flags, bf16[8,16,8,384]{3,2,1,0:T(8,128)(2,1)S(1)} %maximum_maximum_fusion.1.both, f32[192,1]{1,0:T(8,128)S(1)} %copy.16.gain, f32[192,1]{1,0:T(8,128)S(1)} %copy.17.nbias, bf16[576,192]{1,0:T(8,128)(2,1)S(1)} %bitcast.9, ...), custom_call_target="tpu_custom_call" | custom-call | flops 20000000000 | bytes 4000000 | tf_op jit(solution)/shard_map/window_grads/pallas_call | solution.py:176
  56.6 0.1 add.173
  56.8 0.9 collective-permute-start.6
  57.7 1.0 collective-permute-done.6
  58.9 0.1 collective-permute-start.7
  59.0 6.3 %collective-permute-start.9 = (bf16[1,160,128]{2,1,0:T(8,128)(2,1)S(1)}, bf16[1,160,128]{2,1,0:T(8,128)(2,1)S(1)}, u32[]{:S(2)}, u32[]{:S(2)}) collective-permute-start(bf16[1,160,128]{2,1,0:T(8,128)(2,1)S(1)} %get-tuple-element.39), channel_id=1, source_target_pairs={{0,3},{1,2},{2,1},{3,0},{4,7},{5,6},{6,5},{7,4},{8,11},{9,10},{10,... | collective-permute-start | bytes 122888 | tf_op jit(solution)/shard_map/ppermute | solution.py:211
  65.3 0.5 collective-permute-start.8
  65.7 0.0 collective-permute-done.7
  65.8 2.6 %collective-permute-done.8 = bf16[1,160,128]{2,1,0:T(8,128)(2,1)S(1)} collective-permute-done((bf16[1,160,128]{2,1,0:T(8,128)(2,1)S(1)}, bf16[1,160,128]{2,1,0:T(8,128)(2,1)S(1)}, u32[]{:S(2)}, u32[]{:S(2)}) %collective-permute-start.8) | collective-permute-done | bytes 40992 | tf_op jit(solution)/shard_map/ppermute | solution.py:211
  68.6 3.8 %collective-permute-start.12 = (bf16[1,160,128]{2,1,0:T(8,128)(2,1)S(1)}, bf16[1,160,128]{2,1,0:T(8,128)(2,1)S(1)}, u32[]{:S(2)}, u32[]{:S(2)}) collective-permute-start(bf16[1,160,128]{2,1,0:T(8,128)(2,1)S(1)} %get-tuple-element.49), channel_id=1, source_target_pairs={{0,48},{16,32},{32,16},{48,0},{1,49},{17,33},{33,17},{49,1},{2,50}... | collective-permute-start | bytes 122888 | tf_op jit(solution)/shard_map/ppermute | solution.py:211
  72.4 0.1 collective-permute-start.11
  72.5 0.6 collective-permute-start.10
  73.1 0.7 collective-permute-done.12
  73.8 1.9 %collective-permute-done.10 = bf16[1,160,128]{2,1,0:T(8,128)(2,1)S(1)} collective-permute-done((bf16[1,160,128]{2,1,0:T(8,128)(2,1)S(1)}, bf16[1,160,128]{2,1,0:T(8,128)(2,1)S(1)}, u32[]{:S(2)}, u32[]{:S(2)}) %collective-permute-start.10) | collective-permute-done | bytes 40992 | tf_op jit(solution)/shard_map/ppermute | solution.py:211
  75.8 1.1 %collective-permute-done.11 = bf16[1,160,128]{2,1,0:T(8,128)(2,1)S(1)} collective-permute-done((bf16[1,160,128]{2,1,0:T(8,128)(2,1)S(1)}, bf16[1,160,128]{2,1,0:T(8,128)(2,1)S(1)}, u32[]{:S(2)}, u32[]{:S(2)}) %collective-permute-start.11) | collective-permute-done | bytes 40992 | tf_op jit(solution)/shard_map/ppermute | solution.py:211
  77.0 0.1 collective-permute-start.13
  77.1 2.8 %collective-permute-done.13 = bf16[1,160,128]{2,1,0:T(8,128)(2,1)S(1)} collective-permute-done((bf16[1,160,128]{2,1,0:T(8,128)(2,1)S(1)}, bf16[1,160,128]{2,1,0:T(8,128)(2,1)S(1)}, u32[]{:S(2)}, u32[]{:S(2)}) %collective-permute-start.13) | collective-permute-done | bytes 40992 | tf_op jit(solution)/shard_map/ppermute | solution.py:211
  80.1 0.1 collective-permute-start.16
  80.2 0.5 collective-permute-start.15
  80.7 5.5 %collective-permute-start.14 = (bf16[1,160,128]{2,1,0:T(8,128)(2,1)S(1)}, bf16[1,160,128]{2,1,0:T(8,128)(2,1)S(1)}, u32[]{:S(2)}, u32[]{:S(2)}) collective-permute-start(bf16[1,160,128]{2,1,0:T(8,128)(2,1)S(1)} %get-tuple-element.45), channel_id=1, source_target_pairs={{0,128},{4,132},{64,192},{68,196},{128,0},{132,4},{192,64},{196,68... | collective-permute-start | bytes 122888 | tf_op jit(solution)/shard_map/ppermute | solution.py:211
  86.2 0.0 collective-permute-done.16
  86.2 2.3 %collective-permute-done.14 = bf16[1,160,128]{2,1,0:T(8,128)(2,1)S(1)} collective-permute-done((bf16[1,160,128]{2,1,0:T(8,128)(2,1)S(1)}, bf16[1,160,128]{2,1,0:T(8,128)(2,1)S(1)}, u32[]{:S(2)}, u32[]{:S(2)}) %collective-permute-start.14) | collective-permute-done | bytes 40992 | tf_op jit(solution)/shard_map/ppermute | solution.py:211
  88.5 0.0 collective-permute-done.15
  88.7 0.3 collective-permute-start.19
  88.9 2.7 %collective-permute-start.18 = (bf16[1,160,128]{2,1,0:T(8,128)(2,1)S(1)}, bf16[1,160,128]{2,1,0:T(8,128)(2,1)S(1)}, u32[]{:S(2)}, u32[]{:S(2)}) collective-permute-start(bf16[1,160,128]{2,1,0:T(8,128)(2,1)S(1)} %pad_maximum_fusion.10), channel_id=1, source_target_pairs={{0,2},{1,3},{2,0},{3,1},{4,6},{5,7},{6,4},{7,5},{8,10},{9,11},{10,... | collective-permute-start | bytes 122888 | tf_op jit(solution)/shard_map/ppermute | solution.py:211
  91.7 1.0 collective-permute-start.17
  92.6 0.8 collective-permute-done.18
  93.5 2.2 %collective-permute-done.17 = bf16[1,160,128]{2,1,0:T(8,128)(2,1)S(1)} collective-permute-done((bf16[1,160,128]{2,1,0:T(8,128)(2,1)S(1)}, bf16[1,160,128]{2,1,0:T(8,128)(2,1)S(1)}, u32[]{:S(2)}, u32[]{:S(2)}) %collective-permute-start.17) | collective-permute-done | bytes 40992 | tf_op jit(solution)/shard_map/ppermute | solution.py:211
  95.8 6.7 %collective-permute-start.20 = (bf16[4,160,128]{2,1,0:T(8,128)(2,1)S(1)}, bf16[4,160,128]{2,1,0:T(8,128)(2,1)S(1)}, u32[]{:S(2)}, u32[]{:S(2)}) collective-permute-start(bf16[4,160,128]{2,1,0:T(8,128)(2,1)S(1)} %pad_maximum_fusion.6), channel_id=1, source_target_pairs={{0,8},{8,0},{1,9},{9,1},{2,10},{10,2},{3,11},{11,3},{4,12},{12,4},... | collective-permute-start | bytes 491528 | tf_op jit(solution)/shard_map/ppermute | solution.py:211
  102.5 1.2 %pad_maximum_fusion = bf16[8,16,16,192]{3,2,1,0:T(8,128)(2,1)} fusion(bf16[8,16,8,192]{3,2,1,0:T(8,128)(2,1)S(1)} %get-tuple-element.12, bf16[8,16,8,192]{3,2,1,0:T(8,128)(2,1)S(1)} %get-tuple-element.11), kind=kLoop, calls=%fused_computation.13 | loop fusion | flops 1572864 | bytes 1572864 | tf_op jit(solution)/shard_map/concatenate | solution.py:343
  103.9 0.1 maximum_multiply_fusion
  104.0 0.6 fusion.21
  104.6 0.6 slice.395
  105.2 0.1 fusion.20
  105.3 0.0 copy-start.4
  105.3 0.7 pad_maximum_fusion.3
  106.0 0.1 copy-done.4
  (95 shorter events, 1.0 us)
Async XLA Ops:
  0.6 5.3 %copy-start.2 = (bf16[8,16,16,192]{3,2,1,0:T(8,128)(2,1)S(1)}, bf16[8,16,16,192]{3,2,1,0:T(8,128)(2,1)}, u32[]{:S(2)}) copy-start(bf16[8,16,16,192]{3,2,1,0:T(8,128)(2,1)} %param.8) | copy-start | bytes 2359300
  0.6 5.3 %copy-start.3 = (bf16[8,16,16,192]{3,2,1,0:T(8,128)(2,1)S(1)}, bf16[8,16,16,192]{3,2,1,0:T(8,128)(2,1)}, u32[]{:S(2)}) copy-start(bf16[8,16,16,192]{3,2,1,0:T(8,128)(2,1)} %param.7) | copy-start | bytes 2359300
  2.7 10.3 %collective-permute-start = (bf16[8,4,16,384]{3,2,1,0:T(8,128)(2,1)}, bf16[8,4,16,384]{3,2,1,0:T(8,128)(2,1)}, u32[]{:S(2)}, u32[]{:S(2)}) collective-permute-start(bf16[8,4,16,384]{3,2,1,0:T(8,128)(2,1)} %fusion.2), channel_id=1, source_target_pairs={{0,8},{8,0},{1,9},{9,1},{2,10},{10,2},{3,11},{11,3},{4,12},{12,4},... | collective-permute-start | bytes 1179656 | tf_op jit(solution)/shard_map/ppermute | solution.py:289
  6.9 17.7 %collective-permute-start.1 = (bf16[4,12,8,384]{3,2,1,0:T(8,128)(2,1)}, bf16[4,12,8,384]{3,2,1,0:T(8,128)(2,1)}, u32[]{:S(2)}, u32[]{:S(2)}) collective-permute-start(bf16[4,12,8,384]{3,2,1,0:T(8,128)(2,1)} %pad_maximum_fusion.1), channel_id=1, source_target_pairs={{0,240},{16,0},{32,16},{48,32},{64,48},{80,64},{96,80},{112,96},{1... | collective-permute-start | bytes 884744 | tf_op jit(solution)/shard_map/ppermute | solution.py:289
  11.8 0.7 copy-start.6
  11.8 0.8 copy-start.7
  11.8 0.9 copy-start.5
  11.8 1.1 %copy-start = (bf16[192,576]{1,0:T(8,128)(2,1)S(1)}, bf16[192,576]{1,0:T(8,128)(2,1)}, u32[]{:S(2)}) copy-start(bf16[192,576]{1,0:T(8,128)(2,1)} %w_rows.3) | copy-start | bytes 663556
  14.0 10.6 %collective-permute-start.2 = (bf16[4,4,8,384]{3,2,1,0:T(8,128)(2,1)S(1)}, bf16[4,4,8,384]{3,2,1,0:T(8,128)(2,1)S(1)}, u32[]{:S(2)}, u32[]{:S(2)}) collective-permute-start(bf16[4,4,8,384]{3,2,1,0:T(8,128)(2,1)S(1)} %slice.331), channel_id=1, source_target_pairs={{0,240},{16,0},{32,16},{48,32},{64,48},{80,64},{96,80},{112,96},{1... | collective-permute-start | bytes 294920 | tf_op jit(solution)/shard_map/ppermute | solution.py:289
  16.1 22.9 %collective-permute-start.3 = (bf16[4,16,4,384]{3,2,1,0:T(4,128)(2,1)S(1)}, bf16[4,16,4,384]{3,2,1,0:T(4,128)(2,1)S(1)}, u32[]{:S(2)}, u32[]{:S(2)}) collective-permute-start(bf16[4,16,4,384]{3,2,1,0:T(4,128)(2,1)S(1)} %get-tuple-element.22), channel_id=1, source_target_pairs={{0,240},{16,0},{32,16},{48,32},{64,48},{80,64},{96,80},{112,96},{1... | collective-permute-start | bytes 589832 | tf_op jit(solution)/shard_map/ppermute | solution.py:289
  16.4 22.5 %collective-permute-start.5 = (bf16[4,16,4,384]{3,2,1,0:T(4,128)(2,1)S(1)}, bf16[4,16,4,384]{3,2,1,0:T(4,128)(2,1)S(1)}, u32[]{:S(2)}, u32[]{:S(2)}) collective-permute-start(bf16[4,16,4,384]{3,2,1,0:T(4,128)(2,1)S(1)} %get-tuple-element.23), channel_id=1, source_target_pairs={{0,247},{1,240},{2,241},{3,242},{4,243},{5,244},{6,245},{7,246},{1... | collective-permute-start | bytes 589832 | tf_op jit(solution)/shard_map/ppermute | solution.py:299
  20.3 22.4 %collective-permute-start.4 = (bf16[4,16,4,384]{3,2,1,0:T(4,128)(2,1)S(1)}, bf16[4,16,4,384]{3,2,1,0:T(4,128)(2,1)S(1)}, u32[]{:S(2)}, u32[]{:S(2)}) collective-permute-start(bf16[4,16,4,384]{3,2,1,0:T(4,128)(2,1)S(1)} %get-tuple-element.24), channel_id=1, source_target_pairs={{0,7},{1,0},{2,1},{3,2},{4,3},{5,4},{6,5},{7,6},{8,15},{9,8},{10,9... | collective-permute-start | bytes 589832 | tf_op jit(solution)/shard_map/ppermute | solution.py:289
  24.6 1.1 %copy-start.1 = (bf16[192,192]{1,0:T(8,128)(2,1)S(1)}, bf16[192,192]{1,0:T(8,128)(2,1)}, u32[]{:S(2)}) copy-start(bf16[192,192]{1,0:T(8,128)(2,1)} %proj.3) | copy-start | bytes 221188
  56.8 1.9 %collective-permute-start.6 = (bf16[4,160,128]{2,1,0:T(8,128)(2,1)S(1)}, bf16[4,160,128]{2,1,0:T(8,128)(2,1)S(1)}, u32[]{:S(2)}, u32[]{:S(2)}) collective-permute-start(bf16[4,160,128]{2,1,0:T(8,128)(2,1)S(1)} %pad_maximum_fusion.4), channel_id=1, source_target_pairs={{0,8},{8,0},{1,9},{9,1},{2,10},{10,2},{3,11},{11,3},{4,12},{12,4},... | collective-permute-start | bytes 491528 | tf_op jit(solution)/shard_map/ppermute | solution.py:211
  58.9 6.8 %collective-permute-start.7 = (bf16[1,160,128]{2,1,0:T(8,128)(2,1)S(1)}, bf16[1,160,128]{2,1,0:T(8,128)(2,1)S(1)}, u32[]{:S(2)}, u32[]{:S(2)}) collective-permute-start(bf16[1,160,128]{2,1,0:T(8,128)(2,1)S(1)} %get-tuple-element.41), channel_id=1, source_target_pairs={{0,2},{1,3},{2,0},{3,1},{4,6},{5,7},{6,4},{7,5},{8,10},{9,11},{10,... | collective-permute-start | bytes 122888 | tf_op jit(solution)/shard_map/ppermute | solution.py:211
  59.0 9.4 %collective-permute-start.9 = (bf16[1,160,128]{2,1,0:T(8,128)(2,1)S(1)}, bf16[1,160,128]{2,1,0:T(8,128)(2,1)S(1)}, u32[]{:S(2)}, u32[]{:S(2)}) collective-permute-start(bf16[1,160,128]{2,1,0:T(8,128)(2,1)S(1)} %get-tuple-element.39), channel_id=1, source_target_pairs={{0,3},{1,2},{2,1},{3,0},{4,7},{5,6},{6,5},{7,4},{8,11},{9,10},{10,... | collective-permute-start | bytes 122888 | tf_op jit(solution)/shard_map/ppermute | solution.py:211
  65.3 3.1 %collective-permute-start.8 = (bf16[1,160,128]{2,1,0:T(8,128)(2,1)S(1)}, bf16[1,160,128]{2,1,0:T(8,128)(2,1)S(1)}, u32[]{:S(2)}, u32[]{:S(2)}) collective-permute-start(bf16[1,160,128]{2,1,0:T(8,128)(2,1)S(1)} %get-tuple-element.40), channel_id=1, source_target_pairs={{0,1},{1,0},{2,3},{3,2},{4,5},{5,4},{6,7},{7,6},{8,9},{9,8},{10,11... | collective-permute-start | bytes 122888 | tf_op jit(solution)/shard_map/ppermute | solution.py:211
  68.6 5.2 %collective-permute-start.12 = (bf16[1,160,128]{2,1,0:T(8,128)(2,1)S(1)}, bf16[1,160,128]{2,1,0:T(8,128)(2,1)S(1)}, u32[]{:S(2)}, u32[]{:S(2)}) collective-permute-start(bf16[1,160,128]{2,1,0:T(8,128)(2,1)S(1)} %get-tuple-element.49), channel_id=1, source_target_pairs={{0,48},{16,32},{32,16},{48,0},{1,49},{17,33},{33,17},{49,1},{2,50}... | collective-permute-start | bytes 122888 | tf_op jit(solution)/shard_map/ppermute | solution.py:211
  72.4 4.4 %collective-permute-start.11 = (bf16[1,160,128]{2,1,0:T(8,128)(2,1)S(1)}, bf16[1,160,128]{2,1,0:T(8,128)(2,1)S(1)}, u32[]{:S(2)}, u32[]{:S(2)}) collective-permute-start(bf16[1,160,128]{2,1,0:T(8,128)(2,1)S(1)} %get-tuple-element.49), channel_id=1, source_target_pairs={{0,32},{16,48},{32,0},{48,16},{1,33},{17,49},{33,1},{49,17},{2,34}... | collective-permute-start | bytes 122888 | tf_op jit(solution)/shard_map/ppermute | solution.py:211
  72.5 3.2 %collective-permute-start.10 = (bf16[1,160,128]{2,1,0:T(8,128)(2,1)S(1)}, bf16[1,160,128]{2,1,0:T(8,128)(2,1)S(1)}, u32[]{:S(2)}, u32[]{:S(2)}) collective-permute-start(bf16[1,160,128]{2,1,0:T(8,128)(2,1)S(1)} %get-tuple-element.49), channel_id=1, source_target_pairs={{0,16},{16,0},{32,48},{48,32},{1,17},{17,1},{33,49},{49,33},{2,18}... | collective-permute-start | bytes 122888 | tf_op jit(solution)/shard_map/ppermute | solution.py:211
  77.0 2.9 %collective-permute-start.13 = (bf16[1,160,128]{2,1,0:T(8,128)(2,1)S(1)}, bf16[1,160,128]{2,1,0:T(8,128)(2,1)S(1)}, u32[]{:S(2)}, u32[]{:S(2)}) collective-permute-start(bf16[1,160,128]{2,1,0:T(8,128)(2,1)S(1)} %get-tuple-element.47), channel_id=1, source_target_pairs={{0,64},{4,68},{64,0},{68,4},{128,192},{132,196},{192,128},{196,132... | collective-permute-start | bytes 122888 | tf_op jit(solution)/shard_map/ppermute | solution.py:211
  80.1 6.1 %collective-permute-start.16 = (bf16[1,160,128]{2,1,0:T(8,128)(2,1)S(1)}, bf16[1,160,128]{2,1,0:T(8,128)(2,1)S(1)}, u32[]{:S(2)}, u32[]{:S(2)}) collective-permute-start(bf16[1,160,128]{2,1,0:T(8,128)(2,1)S(1)} %get-tuple-element.45), channel_id=1, source_target_pairs={{0,132},{4,128},{64,196},{68,192},{128,4},{132,0},{192,68},{196,64... | collective-permute-start | bytes 122888 | tf_op jit(solution)/shard_map/ppermute | solution.py:211
  80.2 8.3 %collective-permute-start.15 = (bf16[1,160,128]{2,1,0:T(8,128)(2,1)S(1)}, bf16[1,160,128]{2,1,0:T(8,128)(2,1)S(1)}, u32[]{:S(2)}, u32[]{:S(2)}) collective-permute-start(bf16[1,160,128]{2,1,0:T(8,128)(2,1)S(1)} %get-tuple-element.45), channel_id=1, source_target_pairs={{0,4},{4,0},{64,68},{68,64},{128,132},{132,128},{192,196},{196,192... | collective-permute-start | bytes 122888 | tf_op jit(solution)/shard_map/ppermute | solution.py:211
  80.7 7.8 %collective-permute-start.14 = (bf16[1,160,128]{2,1,0:T(8,128)(2,1)S(1)}, bf16[1,160,128]{2,1,0:T(8,128)(2,1)S(1)}, u32[]{:S(2)}, u32[]{:S(2)}) collective-permute-start(bf16[1,160,128]{2,1,0:T(8,128)(2,1)S(1)} %get-tuple-element.45), channel_id=1, source_target_pairs={{0,128},{4,132},{64,192},{68,196},{128,0},{132,4},{192,64},{196,68... | collective-permute-start | bytes 122888 | tf_op jit(solution)/shard_map/ppermute | solution.py:211
  88.7 3.9 %collective-permute-start.19 = (bf16[1,160,128]{2,1,0:T(8,128)(2,1)S(1)}, bf16[1,160,128]{2,1,0:T(8,128)(2,1)S(1)}, u32[]{:S(2)}, u32[]{:S(2)}) collective-permute-start(bf16[1,160,128]{2,1,0:T(8,128)(2,1)S(1)} %pad_maximum_fusion.10), channel_id=1, source_target_pairs={{0,1},{1,0},{2,3},{3,2},{4,5},{5,4},{6,7},{7,6},{8,9},{9,8},{10,11... | collective-permute-start | bytes 122888 | tf_op jit(solution)/shard_map/ppermute | solution.py:211
  88.9 4.5 %collective-permute-start.18 = (bf16[1,160,128]{2,1,0:T(8,128)(2,1)S(1)}, bf16[1,160,128]{2,1,0:T(8,128)(2,1)S(1)}, u32[]{:S(2)}, u32[]{:S(2)}) collective-permute-start(bf16[1,160,128]{2,1,0:T(8,128)(2,1)S(1)} %pad_maximum_fusion.10), channel_id=1, source_target_pairs={{0,2},{1,3},{2,0},{3,1},{4,6},{5,7},{6,4},{7,5},{8,10},{9,11},{10,... | collective-permute-start | bytes 122888 | tf_op jit(solution)/shard_map/ppermute | solution.py:211
  91.7 4.1 %collective-permute-start.17 = (bf16[1,160,128]{2,1,0:T(8,128)(2,1)S(1)}, bf16[1,160,128]{2,1,0:T(8,128)(2,1)S(1)}, u32[]{:S(2)}, u32[]{:S(2)}) collective-permute-start(bf16[1,160,128]{2,1,0:T(8,128)(2,1)S(1)} %pad_maximum_fusion.10), channel_id=1, source_target_pairs={{0,3},{1,2},{2,1},{3,0},{4,7},{5,6},{6,5},{7,4},{8,11},{9,10},{10,... | collective-permute-start | bytes 122888 | tf_op jit(solution)/shard_map/ppermute | solution.py:211
  95.8 7.9 %collective-permute-start.20 = (bf16[4,160,128]{2,1,0:T(8,128)(2,1)S(1)}, bf16[4,160,128]{2,1,0:T(8,128)(2,1)S(1)}, u32[]{:S(2)}, u32[]{:S(2)}) collective-permute-start(bf16[4,160,128]{2,1,0:T(8,128)(2,1)S(1)} %pad_maximum_fusion.6), channel_id=1, source_target_pairs={{0,8},{8,0},{1,9},{9,1},{2,10},{10,2},{3,11},{11,3},{4,12},{12,4},... | collective-permute-start | bytes 491528 | tf_op jit(solution)/shard_map/ppermute | solution.py:211
  105.3 0.8 copy-start.4
